TPU v7x, 512 devices: a whole 4x8x8 slice. The times are simulated.
512 devices in a mesh: wide: 32 (over z_lo, y), narrow: 16 (over x, z_hi, core).
Axes of the slice: x: 4, y: 8, z: 8 (z_hi: 2, z_lo: 4; z = z_hi * 4 + z_lo), core: 2. Of those that a mesh axis runs over, the one named last changes fastest.
Arguments:
- features: bfloat16 [32, 16, 128, 128], P('wide', 'narrow'), may hold values from -6 to 6
- offsets: bfloat16 [32, 16, 2, 128], P('wide', 'narrow'), may hold values from 0 to 1
- counts: int32 [32, 16], P('wide', 'narrow'), may hold values from 64 to 128
- owned_pairs: int32 [32, 16, 8], P('wide', 'narrow'), may hold values from 0 to 1, as said below
- kernels: bfloat16 [8, 128, 128], replicated, may hold values from -0.1875 to 0.1875
- cotangent: bfloat16 [32, 16, 128, 128], P('wide', 'narrow'), may hold values from -6 to 6
Outputs:
- corrected: bfloat16 [32, 16, 128, 128], P('wide', 'narrow')
- grad_features: float32 [32, 16, 128, 128], P('wide', 'narrow')
- grad_kernels: float32 [8, 128, 128], replicated
Inputs may be any that keep to these rules, and one draw needn't show every extreme that they name: owned_pairs[x, y, s] = 1 means that the device of cell (x, y) evaluates the pair of tower cell (x, y + a) and plate cell (x + b, y), indices modulo 32 and 16, with (a, b) the s-th of (0,1), (0,-1), (-1,0), (1,0), (-1,1), (1,-1), (1,1), (-1,-1). Each unordered pair of distinct cells whose indices differ by at most one in each dimension is evaluated at most once, by one of its two candidate devices. Some device evaluates all 8.
All inputs are finite; a program needn't handle non-finite values.
Results may differ from a plain program's by a relative error of at most 0.0075.
Values may be sent and summed in bfloat16 or wider, within the bound.
No kernel may reach another device: no remote copies, remote signals or barrier semaphores. Data moves between devices by JAX's collectives and lax.ppermute only.
A program may use at most 64 MiB of HBM per device.

v0:
```python
import math

import jax
import jax.numpy as jnp
from jax import lax
from jax.sharding import PartitionSpec as P

KERNEL_SCALE = 0.0625
SLOT_SHIFTS = ((0, 1), (0, -1), (-1, 0), (1, 0), (-1, 1), (1, -1), (1, 1), (-1, -1))


def padded(array, sides, width):
    for axis, dim in sides:
        size, length = (lax.axis_size(axis), array.shape[dim])
        up = [(i, (i + 1) % size) for i in range(size)]
        down = [(j, i) for i, j in up]
        last = lax.slice_in_dim(array, length - width, length, axis=dim)
        initial = lax.slice_in_dim(array, 0, width, axis=dim)
        before = lax.ppermute(last, axis, up)
        after = lax.ppermute(initial, axis, down)
        array = jnp.concatenate([before, array, after], axis=dim)
    return array


def shortened(array):

    def short(part):
        return part.astype(jnp.bfloat16) if part.dtype == jnp.float32 else part

    return jax.tree.map(short, array)


def passed_along(value, axis, steps):
    count = lax.axis_size(axis)
    pairs = [(source, (source + steps) % count) for source in range(count)]
    return lax.ppermute(value, axis, pairs)


def kernel_terms(tower_geom, plate_geom, row_shift, col_shift):
    delta_x = plate_geom[..., 0, None, :] + col_shift - tower_geom[..., 0, :, None]
    delta_y = plate_geom[..., 1, None, :] - row_shift - tower_geom[..., 1, :, None]
    square = delta_x * delta_x + delta_y * delta_y
    radius = jnp.sqrt(square)
    window = jnp.square(jnp.maximum(1.0 - square, 0.0))
    weight = KERNEL_SCALE * window * tower_geom[..., 2, :, None] * plate_geom[..., 2, None, :]
    pieces = []
    for level_index in range(4):
        bump_term = weight * jnp.maximum(1.0 - jnp.abs(3.0 * radius - level_index), 0.0)
        pieces.append(bump_term * delta_x)
        pieces.append(bump_term * delta_y)
    return jnp.stack(pieces, axis=-3)


def project(upstream, kernels):
    return jnp.einsum("id,kcd->kic", upstream, kernels, preferred_element_type=jnp.float32).astype(
        jnp.bfloat16
    )


def pack_blocks(members):
    return jnp.concatenate(
        [member.reshape(member.shape[0], member.shape[1], -1) for member in members], axis=2
    )


def pair_terms(tower_block, plate_block, row_shift, col_shift, kernels):
    tower_h, tower_g, tower_geo, tower_proj = tower_block
    plate_h, plate_g, plate_geo, plate_proj = plate_block
    kernel_f32 = kernel_terms(
        tower_geo.astype(jnp.float32), plate_geo.astype(jnp.float32), row_shift, col_shift
    )
    row_sums = jnp.sum(kernel_f32, axis=2)
    col_sums = jnp.sum(kernel_f32, axis=1)
    kernel_half = kernel_f32.astype(jnp.bfloat16)
    tower_mix = (
        row_sums[:, :, None] * tower_h.astype(jnp.float32)[None]
        + jnp.einsum("kij,jc->kic", kernel_half, plate_h, preferred_element_type=jnp.float32)
    ).astype(jnp.bfloat16)
    plate_mix = (
        jnp.einsum("kij,ic->kjc", kernel_half, tower_h, preferred_element_type=jnp.float32)
        + col_sums[:, :, None] * plate_h.astype(jnp.float32)[None]
    ).astype(jnp.bfloat16)
    tower_force = jnp.einsum("kic,kcd->id", tower_mix, kernels, preferred_element_type=jnp.float32)
    plate_force = -jnp.einsum("kjc,kcd->jd", plate_mix, kernels, preferred_element_type=jnp.float32)
    tower_grad = jnp.sum(
        row_sums[:, :, None] * tower_proj.astype(jnp.float32), axis=0
    ) - jnp.einsum("kij,kjc->ic", kernel_half, plate_proj, preferred_element_type=jnp.float32)
    plate_grad = jnp.einsum(
        "kij,kic->jc", kernel_half, tower_proj, preferred_element_type=jnp.float32
    ) - jnp.sum(col_sums[:, :, None] * plate_proj.astype(jnp.float32), axis=0)
    weight_part = jnp.einsum(
        "kic,id->kcd", tower_mix, tower_g, preferred_element_type=jnp.float32
    ) - jnp.einsum("kjc,jd->kcd", plate_mix, plate_g, preferred_element_type=jnp.float32)
    return (jnp.stack([tower_force, tower_grad]), jnp.stack([plate_force, plate_grad]), weight_part)


def body(features, offsets, counts, owned_pairs, kernels, cotangent):
    particles = features.shape[2]
    channels = features.shape[3]
    live_row = (lax.iota(jnp.int32, particles) < counts[0, 0]).astype(jnp.bfloat16)
    geometry = jnp.concatenate([offsets, live_row[None, None, None, :]], axis=2)
    own_proj = project(cotangent[0, 0], kernels)
    payload = (features, cotangent, geometry)
    own_block = (features[0, 0], cotangent[0, 0], geometry[0, 0], own_proj)
    block_len = particles * channels

    def block_at(packed, first, second):
        flat_row = packed[first, second]
        feat_part = flat_row[0:block_len].reshape(particles, channels)
        cot_part = flat_row[block_len : 2 * block_len].reshape(particles, channels)
        geo_end = 2 * block_len + 3 * particles
        geo_part = flat_row[2 * block_len : geo_end].reshape(3, particles)
        proj_part = project(cot_part, kernels)
        return (feat_part, cot_part, geo_part, proj_part)

    zeros_pair = jnp.zeros((2, particles, channels), jnp.float32)
    zeros_weight = jnp.zeros(kernels.shape, jnp.float32)
    packed_own = pack_blocks(payload)
    partial_sums = {
        target: zeros_pair
        for target in ("own", "tower_low", "tower_high", "plate_low", "plate_high")
    }
    weight_list = [zeros_weight]

    def run_slot(slot_index, towers, plates):
        if slot_index < 8:
            row_shift, col_shift = SLOT_SHIFTS[slot_index]
        else:
            row_shift, col_shift = (0, 0)
        tower_block = own_block if row_shift == 0 else towers[row_shift]
        plate_block = own_block if col_shift == 0 else plates[col_shift]

        def evaluate():
            return pair_terms(tower_block, plate_block, row_shift, col_shift, kernels)

        def skipped():
            return (zeros_pair, zeros_pair, zeros_weight)

        if slot_index < 8:
            tower_part, plate_part, weight_part = lax.cond(
                owned_pairs[0, 0, slot_index] > 0, evaluate, skipped
            )
        else:
            tower_part, plate_part, weight_part = evaluate()
        tower_name = "own" if row_shift == 0 else "tower_low" if row_shift < 0 else "tower_high"
        plate_name = "own" if col_shift == 0 else "plate_low" if col_shift < 0 else "plate_high"
        partial_sums[tower_name] = partial_sums[tower_name] + tower_part
        partial_sums[plate_name] = partial_sums[plate_name] + plate_part
        weight_list[0] = weight_list[0] + weight_part

    tower_stacks = padded(packed_own, (("narrow", 1),), 1)
    towers = {-1: block_at(tower_stacks, 0, 0), 1: block_at(tower_stacks, 0, 2)}
    plate_stacks = padded(packed_own, (("wide", 0),), 1)
    plates = {-1: block_at(plate_stacks, 0, 0), 1: block_at(plate_stacks, 2, 0)}
    for slot_index in range(9):
        run_slot(slot_index, towers, plates)
    combined = partial_sums["own"]
    for offset, target in ((1, "tower_high"), (-1, "tower_low")):
        tower_values = partial_sums[target]
        combined = combined + passed_along(shortened(tower_values), "narrow", offset).astype(
            tower_values.dtype
        )
    for offset, target in ((1, "plate_high"), (-1, "plate_low")):
        values = partial_sums[target]
        combined = combined + passed_along(shortened(values), "wide", offset).astype(values.dtype)
    weight_total = weight_list[0]
    weights = lax.psum(weight_total, ("wide", "narrow"))
    normalizer = 1.0 / math.sqrt(lax.axis_size("wide") * lax.axis_size("narrow") * particles)
    corrected = combined[0].astype(jnp.bfloat16)[None, None]
    grad_features = combined[1][None, None]
    return (corrected, grad_features, weights * normalizer)


def solution(mesh):
    placed = (
        P("wide", "narrow", None, None),
        P("wide", "narrow", None, None),
        P("wide", "narrow"),
        P("wide", "narrow", None),
        P(),
        P("wide", "narrow", None, None),
    )
    return jax.shard_map(
        body,
        mesh=mesh,
        in_specs=placed,
        out_specs=(P("wide", "narrow", None, None), P("wide", "narrow", None, None), P()),
        check_vma=False,
    )
```

profile of v0, /device:TPU:1, one launch (start us, length us, event | category | flops | bytes accessed | tf_op | source)
XLA Modules:
  0.0 397.0 jit_solution(17169143389157285740)
XLA Ops:
  10.2 4.0 %collective-permute-start.1 = (bf16[1,1,33152]{2,1,0:T(2,128)(2,1)S(1)}, bf16[1,1,33152]{2,1,0:T(2,128)(2,1)S(1)}, u32[]{:S(2)}, u32[]{:S(2)}) collective-permute-start(bf16[1,1,33152]{2,1,0:T(2,128)(2,1)S(1)} %constant_dynamic-update-slice_fusion), channel_id=1, source_target_pairs={{0,16},{16,32},{32,48},{48,64},{64,80},{80,96},{96,112},{112,128},... | collective-permute-start | bytes 198920 | tf_op jit(solution)/shard_map/ppermute | solution.py:19
  14.2 11.5 %collective-permute-start.2 = (bf16[1,1,33152]{2,1,0:T(2,128)(2,1)S(1)}, bf16[1,1,33152]{2,1,0:T(2,128)(2,1)S(1)}, u32[]{:S(2)}, u32[]{:S(2)}) collective-permute-start(bf16[1,1,33152]{2,1,0:T(2,128)(2,1)S(1)} %constant_dynamic-update-slice_fusion), channel_id=1, source_target_pairs={{0,1},{1,2},{2,3},{3,4},{4,5},{5,6},{6,7},{7,8},{8,9},{9,10},{10,1... | collective-permute-start | bytes 198920 | tf_op jit(solution)/shard_map/ppermute | solution.py:19
  25.7 1.9 collective-permute-start.3
  27.6 6.3 %collective-permute-start = (bf16[1,1,33152]{2,1,0:T(2,128)(2,1)S(1)}, bf16[1,1,33152]{2,1,0:T(2,128)(2,1)S(1)}, u32[]{:S(2)}, u32[]{:S(2)}) collective-permute-start(bf16[1,1,33152]{2,1,0:T(2,128)(2,1)S(1)} %constant_dynamic-update-slice_fusion), channel_id=1, source_target_pairs={{16,0},{32,16},{48,32},{64,48},{80,64},{96,80},{112,96},{128,112},... | collective-permute-start | bytes 198920 | tf_op jit(solution)/shard_map/ppermute | solution.py:20
  36.8 0.9 convolution_bitcast_fusion.35
  38.1 0.9 fusion.395
  39.0 0.9 fusion.397
  39.9 0.9 fusion.393
  50.9 1.4 conditional.9
  52.6 1.9 add_convert_fusion
  54.5 20.8 %collective-permute-start.7 = (bf16[2,128,128]{2,1,0:T(8,128)(2,1)}, bf16[2,128,128]{2,1,0:T(8,128)(2,1)}, u32[]{:S(2)}, u32[]{:S(2)}) collective-permute-start(bf16[2,128,128]{2,1,0:T(8,128)(2,1)} %add_convert_fusion), channel_id=1, source_target_pairs={{0,496},{16,0},{32,16},{48,32},{64,48},{80,64},{96,80},{112,96},{1... | collective-permute-start | bytes 196616 | tf_op jit(solution)/shard_map/ppermute | solution.py:36
  76.9 7.5 %conditional.8 = (f32[2,128,128]{2,1,0:T(8,128)}, f32[2,128,128]{2,1,0:T(8,128)}, f32[8,128,128]{2,1,0:T(8,128)}) conditional(s32[]{:T(128)} %bitcast.144, () %tuple.72, (bf16[3,128]{1,0:T(4,128)(2,1)S(1)}, bf16[3,128]{1,0:T(4,128)(2,1)S(1)}, bf16[128,128]{1,0:T(8,128)(2,1)S(1)}, bf16[128,128]{1,0:T(8,128)(2,1)S(1)}, ...), branch_computations={%region_0.0_spmd, %region_1.0_spmd} | conditional | flops 272841728 | bytes 10218036 | solution.py:140
  76.9 0.8 copy.86
  83.3 1.1 convolution_subtract_fusion
  85.3 1.6 add_convert_fusion.1
  86.9 1.9 collective-permute-start.6
  88.8 9.0 %conditional.10 = (f32[2,128,128]{2,1,0:T(8,128)}, f32[2,128,128]{2,1,0:T(8,128)}, f32[8,128,128]{2,1,0:T(8,128)}) conditional(s32[]{:T(128)} %bitcast.154, () %tuple.76, (bf16[3,128]{1,0:T(4,128)(2,1)S(1)}, bf16[3,128]{1,0:T(4,128)(2,1)S(1)}, bf16[128,128]{1,0:T(8,128)(2,1)S(1)}, bf16[128,128]{1,0:T(8,128)(2,1)S(1)}, ...), branch_computations={%region_12.0_spmd, %region_13.0_spmd} | conditional | flops 272841728 | bytes 9693832 | solution.py:140
  92.4 0.8 copy.88
  93.2 1.2 multiply_reduce_fusion.4
  96.7 1.1 convolution_subtract_fusion.2
  97.8 1.7 add_convert_fusion.2
  99.5 4.0 collective-permute-start.5
  103.5 7.1 %conditional.11 = (f32[2,128,128]{2,1,0:T(8,128)S(1)}, f32[2,128,128]{2,1,0:T(8,128)S(1)}, f32[8,128,128]{2,1,0:T(8,128)}) conditional(s32[]{:T(128)} %bitcast.156, () %tuple.78, (bf16[3,128]{1,0:T(4,128)(2,1)S(1)}, bf16[3,128]{1,0:T(4,128)(2,1)S(1)}, bf16[128,128]{1,0:T(8,128)(2,1)S(1)}, bf16[128,128]{1,0:T(8,128)(2,1)S(1)}, ...), branch_computations={%region_18.0_spmd, %region_19.0_spmd} | conditional | flops 272841728 | bytes 9693748 | solution.py:140
  106.4 0.9 copy.89
  107.3 1.2 multiply_reduce_fusion.6
  109.5 1.1 convolution_subtract_fusion.3
  110.6 0.9 add_convert_fusion.3
  111.5 5.5 %collective-permute-start.4 = (bf16[2,128,128]{2,1,0:T(8,128)(2,1)S(1)}, bf16[2,128,128]{2,1,0:T(8,128)(2,1)S(1)}, u32[]{:S(2)}, u32[]{:S(2)}) collective-permute-start(bf16[2,128,128]{2,1,0:T(8,128)(2,1)S(1)} %add_convert_fusion.3), channel_id=1, source_target_pairs={{0,1},{1,2},{2,3},{3,4},{4,5},{5,6},{6,7},{7,8},{8,9},{9,10},{10,1... | collective-permute-start | bytes 196616 | tf_op jit(solution)/shard_map/ppermute | solution.py:36
  117.0 2.9 fusion.384
  120.9 1.2 fusion.404
  123.3 264.9 %all-reduce.2.cloned.1.call-done = f32[8,128,128]{2,1,0:T(8,128)} async-done(((f32[8,128,128]{2,1,0:T(8,128)}), f32[8,128,128]{2,1,0:T(8,128)}) %all-reduce.2.cloned.1.call-update) | async-done | bytes 524304 | tf_op jit(solution)/shard_map/psum | solution.py:167
  388.2 1.9 broadcast_multiply_fusion
  (220 shorter events, 31.7 us)
Async XLA Ops:
  7.2 381.1 %all-reduce.2.cloned.1.call-start = ((), (), s32[]{:S(2)}) async-start(), calls=%async_computation | async-start | bytes 1048576 | tf_op jit(solution)/shard_map/psum | solution.py:167
  10.1 23.8 %copy-start.1 = (bf16[1,1,128,128]{3,2,1,0:T(8,128)(2,1)S(1)}, bf16[1,1,128,128]{3,2,1,0:T(8,128)(2,1)}, u32[]{:S(2)}) copy-start(bf16[1,1,128,128]{3,2,1,0:T(8,128)(2,1)} %param.22) | copy-start | bytes 98308
  10.2 36.3 %collective-permute-start.1 = (bf16[1,1,33152]{2,1,0:T(2,128)(2,1)S(1)}, bf16[1,1,33152]{2,1,0:T(2,128)(2,1)S(1)}, u32[]{:S(2)}, u32[]{:S(2)}) collective-permute-start(bf16[1,1,33152]{2,1,0:T(2,128)(2,1)S(1)} %constant_dynamic-update-slice_fusion), channel_id=1, source_target_pairs={{0,16},{16,32},{32,48},{48,64},{64,80},{80,96},{96,112},{112,128},... | collective-permute-start | bytes 198920 | tf_op jit(solution)/shard_map/ppermute | solution.py:19
  14.2 34.9 %collective-permute-start.2 = (bf16[1,1,33152]{2,1,0:T(2,128)(2,1)S(1)}, bf16[1,1,33152]{2,1,0:T(2,128)(2,1)S(1)}, u32[]{:S(2)}, u32[]{:S(2)}) collective-permute-start(bf16[1,1,33152]{2,1,0:T(2,128)(2,1)S(1)} %constant_dynamic-update-slice_fusion), channel_id=1, source_target_pairs={{0,1},{1,2},{2,3},{3,4},{4,5},{5,6},{6,7},{7,8},{8,9},{9,10},{10,1... | collective-permute-start | bytes 198920 | tf_op jit(solution)/shard_map/ppermute | solution.py:19
  25.7 21.4 %collective-permute-start.3 = (bf16[1,1,33152]{2,1,0:T(2,128)(2,1)S(1)}, bf16[1,1,33152]{2,1,0:T(2,128)(2,1)S(1)}, u32[]{:S(2)}, u32[]{:S(2)}) collective-permute-start(bf16[1,1,33152]{2,1,0:T(2,128)(2,1)S(1)} %constant_dynamic-update-slice_fusion), channel_id=1, source_target_pairs={{1,0},{2,1},{3,2},{4,3},{5,4},{6,5},{7,6},{8,7},{9,8},{10,9},{11,1... | collective-permute-start | bytes 198920 | tf_op jit(solution)/shard_map/ppermute | solution.py:20
  27.6 20.5 %collective-permute-start = (bf16[1,1,33152]{2,1,0:T(2,128)(2,1)S(1)}, bf16[1,1,33152]{2,1,0:T(2,128)(2,1)S(1)}, u32[]{:S(2)}, u32[]{:S(2)}) collective-permute-start(bf16[1,1,33152]{2,1,0:T(2,128)(2,1)S(1)} %constant_dynamic-update-slice_fusion), channel_id=1, source_target_pairs={{16,0},{32,16},{48,32},{64,48},{80,64},{96,80},{112,96},{128,112},... | collective-permute-start | bytes 198920 | tf_op jit(solution)/shard_map/ppermute | solution.py:20
  35.6 1.0 copy-start
  39.9 0.9 copy-start.44
  46.9 3.3 copy-start.5
  46.9 3.3 copy-start.27
  52.6 22.7 %copy-start.33 = (f32[2,128,128]{2,1,0:T(8,128)}, f32[2,128,128]{2,1,0:T(8,128)S(1)}, u32[]{:S(2)}) copy-start(f32[2,128,128]{2,1,0:T(8,128)S(1)} %get-tuple-element.248) | copy-start | bytes 393220
  52.6 22.7 %copy-start.2 = (f32[8,128,128]{2,1,0:T(8,128)}, f32[8,128,128]{2,1,0:T(8,128)S(1)}, u32[]{:S(2)}) copy-start(f32[8,128,128]{2,1,0:T(8,128)S(1)} %get-tuple-element.264) | copy-start | bytes 1572868
  52.6 22.7 %copy-start.18 = (bf16[16384]{0:T(1024)(128)(2,1)S(1)}, bf16[16384]{0:T(1024)(128)(2,1)}, u32[]{:S(2)}) copy-start(bf16[16384]{0:T(1024)(128)(2,1)} %copy-done.17) | copy-start | bytes 98308
  52.6 22.7 %copy-start.26 = (bf16[16384]{0:T(1024)(128)(2,1)S(1)}, bf16[16384]{0:T(1024)(128)(2,1)}, u32[]{:S(2)}) copy-start(bf16[16384]{0:T(1024)(128)(2,1)} %copy-done.25) | copy-start | bytes 98308
  54.5 65.5 %collective-permute-start.7 = (bf16[2,128,128]{2,1,0:T(8,128)(2,1)}, bf16[2,128,128]{2,1,0:T(8,128)(2,1)}, u32[]{:S(2)}, u32[]{:S(2)}) collective-permute-start(bf16[2,128,128]{2,1,0:T(8,128)(2,1)} %add_convert_fusion), channel_id=1, source_target_pairs={{0,496},{16,0},{32,16},{48,32},{64,48},{80,64},{96,80},{112,96},{1... | collective-permute-start | bytes 196616 | tf_op jit(solution)/shard_map/ppermute | solution.py:36
  76.0 0.9 copy-start.35
  76.0 0.9 copy-start.36
  76.0 8.4 %copy-start.22 = (bf16[16384]{0:T(1024)(128)(2,1)S(1)}, bf16[16384]{0:T(1024)(128)(2,1)}, u32[]{:S(2)}) copy-start(bf16[16384]{0:T(1024)(128)(2,1)} %copy-done.21) | copy-start | bytes 98308
  78.9 1.0 copy-start.16
  84.4 0.9 copy-start.37
  84.5 4.3 %copy-start.38 = (f32[2,128,128]{2,1,0:T(8,128)}, f32[2,128,128]{2,1,0:T(8,128)S(1)}, u32[]{:S(2)}) copy-start(f32[2,128,128]{2,1,0:T(8,128)S(1)} %get-tuple-element.251) | copy-start | bytes 393220
  84.5 4.3 %copy-start.4 = (f32[8,128,128]{2,1,0:T(8,128)}, f32[8,128,128]{2,1,0:T(8,128)S(1)}, u32[]{:S(2)}) copy-start(f32[8,128,128]{2,1,0:T(8,128)S(1)} %get-tuple-element.263) | copy-start | bytes 1572868
  86.9 33.1 %collective-permute-start.6 = (bf16[2,128,128]{2,1,0:T(8,128)(2,1)}, bf16[2,128,128]{2,1,0:T(8,128)(2,1)}, u32[]{:S(2)}, u32[]{:S(2)}) collective-permute-start(bf16[2,128,128]{2,1,0:T(8,128)(2,1)} %add_convert_fusion.1), channel_id=1, source_target_pairs={{0,16},{16,32},{32,48},{48,64},{64,80},{80,96},{96,112},{112,128},... | collective-permute-start | bytes 196616 | tf_op jit(solution)/shard_map/ppermute | solution.py:36
  97.8 5.7 %copy-start.11 = (bf16[1,1,128,128]{3,2,1,0:T(8,128)(2,1)S(1)}, bf16[1,1,128,128]{3,2,1,0:T(8,128)(2,1)}, u32[]{:S(2)}) copy-start(bf16[1,1,128,128]{3,2,1,0:T(8,128)(2,1)} %param.27) | copy-start | bytes 98308
  97.8 5.7 %copy-start.19 = (bf16[16384]{0:T(1024)(128)(2,1)S(1)}, bf16[16384]{0:T(1024)(128)(2,1)}, u32[]{:S(2)}) copy-start(bf16[16384]{0:T(1024)(128)(2,1)} %copy-done.17) | copy-start | bytes 98308
  99.5 20.5 %collective-permute-start.5 = (bf16[2,128,128]{2,1,0:T(8,128)(2,1)}, bf16[2,128,128]{2,1,0:T(8,128)(2,1)S(1)}, u32[]{:S(2)}, u32[]{:S(2)}) collective-permute-start(bf16[2,128,128]{2,1,0:T(8,128)(2,1)} %add_convert_fusion.2), channel_id=1, source_target_pairs={{0,15},{1,0},{2,1},{3,2},{4,3},{5,4},{6,5},{7,6},{8,7},{9,8},{10,9... | collective-permute-start | bytes 196616 | tf_op jit(solution)/shard_map/ppermute | solution.py:36
  103.5 7.1 %copy-start.34 = (f32[2,128,128]{2,1,0:T(8,128)S(1)}, f32[2,128,128]{2,1,0:T(8,128)}, u32[]{:S(2)}) copy-start(f32[2,128,128]{2,1,0:T(8,128)} %copy-done.33) | copy-start | bytes 393220
  109.5 1.1 copy-start.39
  111.5 8.5 %collective-permute-start.4 = (bf16[2,128,128]{2,1,0:T(8,128)(2,1)S(1)}, bf16[2,128,128]{2,1,0:T(8,128)(2,1)S(1)}, u32[]{:S(2)}, u32[]{:S(2)}) collective-permute-start(bf16[2,128,128]{2,1,0:T(8,128)(2,1)S(1)} %add_convert_fusion.3), channel_id=1, source_target_pairs={{0,1},{1,2},{2,3},{3,4},{4,5},{5,6},{6,7},{7,8},{8,9},{9,10},{10,1... | collective-permute-start | bytes 196616 | tf_op jit(solution)/shard_map/ppermute | solution.py:36
  119.9 0.9 copy-start.41
  119.9 0.9 copy-start.42
  119.9 0.9 copy-start.43
  (15 other events, 10.4 us)
Sparse Core Ops, SparseCore 0:
  120.1 268.0 all-reduce.1
where the time goes:
time: 399 us; the launch traced here: 397 us
  waiting for transfers between devices  265 us (66%)
  starting transfers between devices  55.8 us (14%)
  other arithmetic  20.4 us (5%)
  between operations  20.4 us (5%)
  local copies, waits for them, and re-layouts  17.6 us (4%)
  matrix products  16.7 us (4%)
    psum x1, waiting for transfers between devices, body(): weights = lax.psum(weight_total, ('wide', 'narrow'))  265 us
    ppermute x4, starting transfers between devices, passed_along(): return lax.ppermute(value, axis, pairs)  32.1 us
    ppermute x2, starting transfers between devices, padded(): before = lax.ppermute(last, axis, up)  15.5 us
    ppermute x2, starting transfers between devices, padded(): after = lax.ppermute(initial, axis, down)  8.18 us
  transfers between devices with their start and end apart: 9, of which 1 were waited for; matrix products, arithmetic and copies ran while one was open for 10% of the time, Pallas kernels for 0%

commit v1 on v0

v1 whole, which is shorter than its diff:
```python
import jax
import jax.numpy as jnp
from jax import lax
from jax.experimental import pallas as pl
from jax.experimental.pallas import tpu as pltpu
from jax.sharding import Mesh, PartitionSpec as P

SLOT_SHIFTS = ((0, 1), (0, -1), (-1, 0), (1, 0), (-1, 1), (1, -1), (1, 1), (-1, -1))
SLOT = {shift: index for index, shift in enumerate(SLOT_SHIFTS)}
KERNEL_SCALE = 0.0625
FAR = 64.0
K, N, C = 8, 128, 128
GEO = 2 * N
ROWS = 2 * N + 16
LIVE, FLAG = GEO + 2, GEO + 3
WIDE = ("zl", "y")
NARROW = ("x", "zh", "core")
GROUP = ("y", "x", "core")
DEPTH = ("zl", "zh")
BF16, F32 = jnp.bfloat16, jnp.float32


def pack_kernel(counts, owned, features, cotangent, offsets, out):
    out[0:N, :] = features[...]
    out[N:GEO, :] = cotangent[...]
    row = lax.broadcasted_iota(jnp.int32, (16, N), 0)
    lane = lax.broadcasted_iota(jnp.int32, (16, N), 1)
    off = offsets[...].astype(F32)
    geo = jnp.where(row == 0, off[0:1, :], jnp.where(row == 1, off[1:2, :], 0.0))
    geo = jnp.where((row == 2) & (lane < counts[0, 0]), 1.0, geo)
    for s in range(8):
        geo = jnp.where(row == 3 + s, owned[0, s].astype(F32), geo)
    out[GEO:ROWS, :] = geo.astype(BF16)


def pack(counts, owned, features, cotangent, offsets):
    smem = pl.BlockSpec(memory_space=pltpu.SMEM)
    vmem = pl.BlockSpec(memory_space=pltpu.VMEM)
    return pl.pallas_call(
        pack_kernel,
        out_shape=jax.ShapeDtypeStruct((ROWS, C), BF16),
        in_specs=[smem, smem, vmem, vmem, vmem],
        out_specs=vmem,
        name="pack",
    )(counts, owned, features, cotangent, offsets)


def pair_kernel(middle, left, right, kernels, corrected, grad, part, s_ref, x_ref, r_ref, t_ref, z_ref, w_ref, p_ref):
    columns = {0: middle, -1: left, 1: right}
    base = {0: 0, 1: ROWS, -1: 2 * ROWS}

    def geo(dx, dy, row):
        at = base[dy] + row
        return columns[dx][at : at + 1, :].astype(F32)

    cells = [(0, 0)] + [(dx, dy) for dx in (0, -1, 1) for dy in (0, 1, -1) if dx or dy]
    for n, (dx, dy) in enumerate(cells):
        use = geo(dx, dy, LIVE)
        if dx or dy:
            use = use * (geo(0, dy, FLAG + SLOT[(-dy, dx)]) + geo(dx, 0, FLAG + SLOT[(dy, -dx)]))
        px = jnp.where(use > 0.5, geo(dx, dy, GEO) + dx, -FAR)
        py = geo(dx, dy, GEO + 1) + dy
        p_ref[2 * n : 2 * n + 1, :] = px
        p_ref[2 * n + 1 : 2 * n + 2, :] = py
        source, at = columns[dx], base[dy]
        x_ref[n * N : (n + 1) * N, 0:C] = source[at : at + N, :]
        x_ref[n * N : (n + 1) * N, C : 2 * C] = source[at + N : at + GEO, :]

    own_x = jnp.where(geo(0, 0, LIVE) > 0.5, geo(0, 0, GEO), FAR)
    own_y = geo(0, 0, GEO + 1)
    t_ref[0:N, 0:N] = jnp.broadcast_to(own_x, (N, N)).T
    t_ref[0:N, N : 2 * N] = jnp.broadcast_to(own_y, (N, N)).T

    def rows(step, carry):
        at = pl.multiple_of(step * 16, 16)
        ax = t_ref[pl.ds(at, 16), 0:N]
        ay = t_ref[pl.ds(at, 16), N : 2 * N]
        sums = [None] * K
        for n in range(len(cells)):
            u = p_ref[2 * n : 2 * n + 1, :] - ax
            v = p_ref[2 * n + 1 : 2 * n + 2, :] - ay
            square = u * u + v * v
            t = square * (3.0 * lax.rsqrt(jnp.maximum(square, 1e-30)))
            low = jnp.maximum(1.0 - square, 0.0)
            window = low * low
            if n == 0:
                window = window + window
            hats = (
                jnp.maximum(1.0 - t, 0.0),
                jnp.maximum(jnp.minimum(t, 2.0 - t), 0.0),
                jnp.maximum(jnp.minimum(t - 1.0, 3.0 - t), 0.0),
                jnp.maximum(t - 2.0, 0.0),
            )
            for q in range(4):
                weight = window * hats[q]
                for k, term in ((2 * q, weight * u), (2 * q + 1, weight * v)):
                    sums[k] = term if n == 0 else sums[k] + term
                    s_ref[pl.ds(k * N + at, 16), n * N : (n + 1) * N] = term.astype(BF16)
        for k in range(K):
            total = jnp.sum(sums[k], axis=1, keepdims=True)
            r_ref[pl.ds(k * N + at, 16), :] = jnp.broadcast_to(total, (16, N))
        return carry

    lax.fori_loop(0, N // 16, rows, 0)

    t_ref[...] = jnp.dot(s_ref[...], x_ref[...], preferred_element_type=F32)
    f = middle[0:N, :].astype(F32)
    g = middle[N:GEO, :].astype(F32)
    for k in range(K):
        r = r_ref[k * N : (k + 1) * N, :]
        z_ref[:, k * C : (k + 1) * C] = (r * f + t_ref[k * N : (k + 1) * N, 0:C]).astype(BF16)
        w_ref[:, k * C : (k + 1) * C] = (r * g - t_ref[k * N : (k + 1) * N, C : 2 * C]).astype(BF16)
    own_g = middle[N:GEO, :]
    part[...] = lax.dot_general(z_ref[...], own_g, (((0,), (0,)), ((), ())), preferred_element_type=F32).astype(BF16)
    force = jnp.dot(z_ref[...], kernels[...], preferred_element_type=F32)
    corrected[...] = (force * KERNEL_SCALE).astype(BF16)
    total = None
    for k in range(K):
        term = lax.dot_general(
            w_ref[:, k * C : (k + 1) * C],
            kernels[k * C : (k + 1) * C, :],
            (((1,), (1,)), ((), ())),
            preferred_element_type=F32,
        )
        total = term if total is None else total + term
    grad[...] = total * KERNEL_SCALE


def evaluate(middle, left, right, kernels):
    vmem = pl.BlockSpec(memory_space=pltpu.VMEM)
    return pl.pallas_call(
        pair_kernel,
        out_shape=(
            jax.ShapeDtypeStruct((N, C), BF16),
            jax.ShapeDtypeStruct((N, C), F32),
            jax.ShapeDtypeStruct((K * C, C), BF16),
        ),
        in_specs=[vmem] * 4,
        out_specs=(vmem,) * 3,
        scratch_shapes=[
            pltpu.VMEM((K * N, 9 * N), BF16),
            pltpu.VMEM((9 * N, 2 * C), BF16),
            pltpu.VMEM((K * N, N), F32),
            pltpu.VMEM((K * N, 2 * C), F32),
            pltpu.VMEM((N, K * C), BF16),
            pltpu.VMEM((N, K * C), BF16),
            pltpu.VMEM((24, N), F32),
        ],
        name="pairs",
    )(middle, left, right, kernels)


def shifted(value, axes, steps):
    count = lax.axis_size(axes)
    return lax.ppermute(value, axes, [(source, (source + steps) % count) for source in range(count)])


def exchanged(blocks, axes):
    return lax.all_to_all(blocks, axes, 0, 0, tiled=False)


def added(blocks):
    return jnp.sum(blocks.astype(F32), axis=0).astype(BF16)


def whole_sum(part):
    group, depth = lax.axis_size(GROUP), lax.axis_size(DEPTH)
    piece = added(exchanged(part.reshape(group, -1, C), GROUP))
    piece = added(exchanged(jnp.broadcast_to(piece, (depth,) + piece.shape), DEPTH))
    return exchanged(jnp.broadcast_to(piece, (group,) + piece.shape), GROUP).reshape(K, C, C)


def body(features, offsets, counts, owned_pairs, kernels, cotangent):
    own = pack(counts, owned_pairs[0], features[0, 0], cotangent[0, 0], offsets[0, 0])
    below, above = shifted(own, NARROW, 1), shifted(own, NARROW, -1)
    middle = jnp.concatenate([own, above, below])
    left, right = shifted(middle, WIDE, 1), shifted(middle, WIDE, -1)
    corrected, grad, part = evaluate(middle, left, right, kernels.reshape(K * C, C))
    scale = KERNEL_SCALE / float(lax.axis_size(WIDE) * lax.axis_size(NARROW) * N) ** 0.5
    weights = whole_sum(part).astype(F32) * scale
    return corrected[None, None], grad[None, None], weights


def solution(mesh):
    split = Mesh(mesh.devices.reshape(4, 8, 4, 2, 2), ("zl", "y", "x", "zh", "core"))
    cell = P(WIDE, NARROW)
    return jax.shard_map(
        body,
        mesh=split,
        in_specs=(cell, cell, cell, cell, P(), cell),
        out_specs=(cell, cell, P()),
        check_vma=False,
    )
```

time: 399 us -> 99.8 us (0.25)
  waiting for transfers between devices: 265 us -> 16.4 us
  blocking collectives: 0 us -> 48.2 us
  starting transfers between devices: 55.8 us -> 23.9 us
  between operations: 20.4 us -> 1.35 us
  other arithmetic: 20.4 us -> 1.81 us
  local copies, waits for them, and re-layouts: 17.6 us -> 0.73 us
  matrix products: 16.7 us -> 0 us
  Pallas kernels: 0 us -> 6.91 us
    psum x1 -> x0, waiting for transfers between devices: 265 us -> none  [body(): weights = lax.psum(weight_total, ('wide', 'narrow'))]
    all_to_all x0 -> x3, blocking collectives: none -> 48.2 us  [exchanged(): return lax.all_to_all(blocks, axes, 0, 0, tiled=False)]
    ppermute x8 -> x4, starting transfers between devices: 55.8 us -> 23.9 us  [shifted(): lax.ppermute(value, axes, [(source, (source + steps) % count) for source...]
    dot_general x37 -> x0, matrix products: 16.7 us -> none  [the longest x4 6.11 us: pair_terms(): jnp.einsum('kjc,jd->kcd', plate_mix, plate_g, preferred_element_type=jnp....]
    ppermute x8 -> x4, waiting for transfers between devices: 0.02 us -> 16.4 us  [shifted(): lax.ppermute(value, axes, [(source, (source + steps) % count) for source...]
    pallas_call x0 -> x2, Pallas kernels: none -> 6.91 us  [the longest x1 5.47 us: evaluate(): pl.pallas_call(pair_kernel, out_shape=(jax.ShapeDtypeStruct((N, C), BF16)...]
    unnamed x66 -> x6, local copies, waits for them, and re-layouts: 7.12 us -> 0.68 us
    convert_element_type x18 -> x0, other arithmetic: 6.1 us -> none  [the longest x4 6.02 us: short(): return part.astype(jnp.bfloat16) if part.dtype == jnp.float32 else part]
  transfers between devices with their start and end apart: 9 -> 4, of which waited for: 1 -> 4; matrix products, arithmetic and copies ran while one was open for 10% -> 0% of each run, Pallas kernels for 0% -> 0%
where the time goes in v1:
time: 99.8 us; the launch traced here: 99.3 us
  blocking collectives  48.2 us (48%)
  starting transfers between devices  23.9 us (24%)
  waiting for transfers between devices  16.4 us (16%)
  Pallas kernels  6.91 us (7%)
  other arithmetic  1.81 us (2%)
  between operations  1.35 us (1%)
    all_to_all x3, blocking collectives, exchanged(): return lax.all_to_all(blocks, axes, 0, 0, tiled=False)  48.2 us
    ppermute x4, starting transfers between devices, shifted(): lax.ppermute(value, axes, [(source, (source + steps) % count) for source...  23.9 us
    ppermute x4, waiting for transfers between devices, shifted(): lax.ppermute(value, axes, [(source, (source + steps) % count) for source...  16.4 us
    pallas_call x1, Pallas kernels, evaluate(): pl.pallas_call(pair_kernel, out_shape=(jax.ShapeDtypeStruct((N, C), BF16)...  5.47 us
  transfers between devices with their start and end apart: 4, of which 4 were waited for; matrix products, arithmetic and copies ran while one was open for 0% of the time, Pallas kernels for 0%

profile of v1, /device:TPU:1, one launch (start us, length us, event | category | flops | bytes accessed | tf_op | source)
XLA Modules:
  0.0 99.3 jit_solution(5229995818240255552)
XLA Ops:
  1.3 1.4 %pack.1 = bf16[272,128]{1,0:T(8,128)(2,1)} custom-call(s32[1,1]{1,0:T(1,128)S(6)} %copy.9.counts, s32[1,8]{1,0:T(1,128)} %bitcast.14, bf16[128,128]{1,0:T(8,128)(2,1)} %bitcast.12, bf16[128,128]{1,0:T(8,128)(2,1)} %bitcast.13, bf16[2,128]{1,0:T(2,128)(2,1)} %bitcast.15), custom_call_target="tpu_custom_call" | custom-call | tf_op jit(solution)/shard_map/pack/pallas_call | solution.py:39
  2.7 12.0 %collective-permute-start.1 = (bf16[272,128]{1,0:T(8,128)(2,1)}, bf16[272,128]{1,0:T(8,128)(2,1)S(1)}, u32[]{:S(2)}, u32[]{:S(2)}) collective-permute-start(bf16[272,128]{1,0:T(8,128)(2,1)} %pack.1), channel_id=1, source_target_pairs={{0,1},{1,2},{2,3},{3,4},{4,5},{5,6},{6,7},{7,8},{8,9},{9,10},{10,1... | collective-permute-start | bytes 208904 | tf_op jit(solution)/shard_map/ppermute | solution.py:155
  14.7 1.9 %collective-permute-start = (bf16[272,128]{1,0:T(8,128)(2,1)}, bf16[272,128]{1,0:T(8,128)(2,1)S(1)}, u32[]{:S(2)}, u32[]{:S(2)}) collective-permute-start(bf16[272,128]{1,0:T(8,128)(2,1)} %pack.1), channel_id=1, source_target_pairs={{0,15},{1,0},{2,1},{3,2},{4,3},{5,4},{6,5},{7,6},{8,7},{9,8},{10,9... | collective-permute-start | bytes 208904 | tf_op jit(solution)/shard_map/ppermute | solution.py:155
  16.7 0.3 collective-permute-done.1
  16.9 7.6 %collective-permute-done = bf16[272,128]{1,0:T(8,128)(2,1)S(1)} collective-permute-done((bf16[272,128]{1,0:T(8,128)(2,1)}, bf16[272,128]{1,0:T(8,128)(2,1)S(1)}, u32[]{:S(2)}, u32[]{:S(2)}) %collective-permute-start) | collective-permute-done | bytes 69664 | tf_op jit(solution)/shard_map/ppermute | solution.py:155
  24.6 0.9 pad_maximum_fusion.middle
  25.5 0.0 copy-start
  25.5 8.0 %collective-permute-start.3 = (bf16[816,128]{1,0:T(8,128)(2,1)S(1)}, bf16[816,128]{1,0:T(8,128)(2,1)S(1)}, u32[]{:S(2)}, u32[]{:S(2)}) collective-permute-start(bf16[816,128]{1,0:T(8,128)(2,1)S(1)} %pad_maximum_fusion.middle), channel_id=1, source_target_pairs={{0,496},{16,0},{32,16},{48,32},{64,48},{80,64},{96,80},{112,96},{1... | collective-permute-start | bytes 626696 | tf_op jit(solution)/shard_map/ppermute | solution.py:155
  33.5 1.9 %collective-permute-start.2 = (bf16[816,128]{1,0:T(8,128)(2,1)S(1)}, bf16[816,128]{1,0:T(8,128)(2,1)S(1)}, u32[]{:S(2)}, u32[]{:S(2)}) collective-permute-start(bf16[816,128]{1,0:T(8,128)(2,1)S(1)} %pad_maximum_fusion.middle), channel_id=1, source_target_pairs={{0,16},{16,32},{32,48},{48,64},{64,80},{80,96},{96,112},{112,128},... | collective-permute-start | bytes 626696 | tf_op jit(solution)/shard_map/ppermute | solution.py:155
  35.4 0.8 collective-permute-done.3.right
  36.2 0.0 copy-start.1
  36.2 7.7 %collective-permute-done.2.left = bf16[816,128]{1,0:T(8,128)(2,1)S(1)} collective-permute-done((bf16[816,128]{1,0:T(8,128)(2,1)S(1)}, bf16[816,128]{1,0:T(8,128)(2,1)S(1)}, u32[]{:S(2)}, u32[]{:S(2)}) %collective-permute-start.2) | collective-permute-done | bytes 208928 | tf_op jit(solution)/shard_map/ppermute | solution.py:155
  44.0 0.0 copy-start.2
  44.0 0.0 copy-done
  44.0 0.0 copy-done.1
  44.0 0.7 copy-done.2
  44.6 5.5 %pairs.1 = (bf16[128,128]{1,0:T(8,128)(2,1)}, f32[128,128]{1,0:T(8,128)}, bf16[1024,128]{1,0:T(8,128)(2,1)}) custom-call(bf16[816,128]{1,0:T(8,128)(2,1)} %copy-done, bf16[816,128]{1,0:T(8,128)(2,1)} %copy-done.2, bf16[816,128]{1,0:T(8,128)(2,1)} %copy-done.1, bf16[1024,128]{1,0:T(8,128)(2,1)} %bitcast.10), custom_call_target="tpu_custom_call" | custom-call | tf_op jit(solution)/shard_map/pairs/pallas_call | solution.py:131
  50.1 17.8 %all_to_all.15 = bf16[64,16,128]{2,1,0:T(8,128)(2,1)S(1)} all-to-all(bf16[64,16,128]{2,1,0:T(8,128)(2,1)} %bitcast.11), channel_id=1, replica_groups=mesh['zl'=4,'y'=8,'x'=4,'zh'=2,'core'=2] {'y','x','core'}, dimensions={0} | all-to-all | bytes 524288 | tf_op jit(solution)/shard_map/all_to_all | solution.py:159
  67.9 0.1 reduce_sum.24
  68.0 11.3 %all_to_all.16 = bf16[8,16,128]{2,1,0:T(8,128)(2,1)S(1)} all-to-all(bf16[8,16,128]{2,1,0:T(8,128)(2,1)S(1)} %broadcast_in_dim.14), channel_id=1, replica_groups=mesh['zl'=4,'y'=8,'x'=4,'zh'=2,'core'=2] {'zl','zh'}, dimensions={0} | all-to-all | bytes 65536 | tf_op jit(solution)/shard_map/all_to_all | solution.py:159
  79.4 19.1 %all_to_all.17 = bf16[64,16,128]{2,1,0:T(8,128)(2,1)S(1)} all-to-all(bf16[64,16,128]{2,1,0:T(8,128)(2,1)S(1)} %broadcast_in_dim.15), channel_id=1, replica_groups=mesh['zl'=4,'y'=8,'x'=4,'zh'=2,'core'=2] {'y','x','core'}, dimensions={0} | all-to-all | bytes 524288 | tf_op jit(solution)/shard_map/all_to_all | solution.py:159
  98.4 0.8 convert_multiply_fusion
  (3 shorter events, 0.1 us)
Async XLA Ops:
  2.7 14.2 %collective-permute-start.1 = (bf16[272,128]{1,0:T(8,128)(2,1)}, bf16[272,128]{1,0:T(8,128)(2,1)S(1)}, u32[]{:S(2)}, u32[]{:S(2)}) collective-permute-start(bf16[272,128]{1,0:T(8,128)(2,1)} %pack.1), channel_id=1, source_target_pairs={{0,1},{1,2},{2,3},{3,4},{4,5},{5,6},{6,7},{7,8},{8,9},{9,10},{10,1... | collective-permute-start | bytes 208904 | tf_op jit(solution)/shard_map/ppermute | solution.py:155
  14.7 9.8 %collective-permute-start = (bf16[272,128]{1,0:T(8,128)(2,1)}, bf16[272,128]{1,0:T(8,128)(2,1)S(1)}, u32[]{:S(2)}, u32[]{:S(2)}) collective-permute-start(bf16[272,128]{1,0:T(8,128)(2,1)} %pack.1), channel_id=1, source_target_pairs={{0,15},{1,0},{2,1},{3,2},{4,3},{5,4},{6,5},{7,6},{8,7},{9,8},{10,9... | collective-permute-start | bytes 208904 | tf_op jit(solution)/shard_map/ppermute | solution.py:155
  25.5 18.5 %copy-start = (bf16[816,128]{1,0:T(8,128)(2,1)}, bf16[816,128]{1,0:T(8,128)(2,1)S(1)}, u32[]{:S(2)}) copy-start(bf16[816,128]{1,0:T(8,128)(2,1)S(1)} %pad_maximum_fusion.middle) | copy-start | bytes 626692
  25.5 10.8 %collective-permute-start.3 = (bf16[816,128]{1,0:T(8,128)(2,1)S(1)}, bf16[816,128]{1,0:T(8,128)(2,1)S(1)}, u32[]{:S(2)}, u32[]{:S(2)}) collective-permute-start(bf16[816,128]{1,0:T(8,128)(2,1)S(1)} %pad_maximum_fusion.middle), channel_id=1, source_target_pairs={{0,496},{16,0},{32,16},{48,32},{64,48},{80,64},{96,80},{112,96},{1... | collective-permute-start | bytes 626696 | tf_op jit(solution)/shard_map/ppermute | solution.py:155
  33.5 10.5 %collective-permute-start.2 = (bf16[816,128]{1,0:T(8,128)(2,1)S(1)}, bf16[816,128]{1,0:T(8,128)(2,1)S(1)}, u32[]{:S(2)}, u32[]{:S(2)}) collective-permute-start(bf16[816,128]{1,0:T(8,128)(2,1)S(1)} %pad_maximum_fusion.middle), channel_id=1, source_target_pairs={{0,16},{16,32},{32,48},{48,64},{64,80},{80,96},{96,112},{112,128},... | collective-permute-start | bytes 626696 | tf_op jit(solution)/shard_map/ppermute | solution.py:155
  36.2 7.7 %copy-start.1 = (bf16[816,128]{1,0:T(8,128)(2,1)}, bf16[816,128]{1,0:T(8,128)(2,1)S(1)}, u32[]{:S(2)}) copy-start(bf16[816,128]{1,0:T(8,128)(2,1)S(1)} %collective-permute-done.3.right) | copy-start | bytes 626692
  44.0 0.7 copy-start.2

commit v2 on v1

v2 whole, which is shorter than its diff:
```python
import jax
import jax.numpy as jnp
from jax import lax
from jax.experimental import pallas as pl
from jax.experimental.pallas import tpu as pltpu
from jax.sharding import Mesh, PartitionSpec as P


SLOT_SHIFTS = ((0, 1), (0, -1), (-1, 0), (1, 0), (-1, 1), (1, -1), (1, 1), (-1, -1))
SLOT = {shift: index for index, shift in enumerate(SLOT_SHIFTS)}
KERNEL_SCALE = 0.0625
FAR = 64.0
K, N, C = 8, 128, 128
GEO = 2 * N
ROWS = 2 * N + 16
HALF = K * C // 2
LIVE, FLAG, SIDES = GEO + 2, GEO + 3, GEO + 11
WIDE = ("zl", "y")
NARROW = ("x", "zh", "core")
GROUP = ("y", "x")
DEPTH = ("zl", "zh")
BF16, F32 = jnp.bfloat16, jnp.float32
HERE = pl.BlockSpec(memory_space=pltpu.VMEM)
LIMIT = pltpu.CompilerParams(vmem_limit_bytes=16 << 20)


def held(value):
    return pltpu.with_memory_space_constraint(value, pltpu.VMEM)


def pack_kernel(counts, owned_hbm, features, cotangent, offsets, out, owned, off_ref, sems):
    copies = (
        pltpu.make_async_copy(offsets, off_ref, sems.at[0]),
        pltpu.make_async_copy(features, out.at[0:N], sems.at[1]),
        pltpu.make_async_copy(cotangent, out.at[N:GEO], sems.at[2]),
        pltpu.make_async_copy(owned_hbm, owned, sems.at[3]),
    )
    for copy in copies:
        copy.start()
    row = lax.broadcasted_iota(jnp.int32, (16, N), 0)
    lane = lax.broadcasted_iota(jnp.int32, (16, N), 1)
    copies[0].wait()
    copies[3].wait()
    off = off_ref[...].astype(F32)
    geo = jnp.where(row == 0, off[0:1, :], jnp.where(row == 1, off[1:2, :], 0.0))
    geo = jnp.where((row == 2) & (lane < counts[0, 0]), 1.0, geo)
    for s in range(8):
        geo = jnp.where(row == 3 + s, owned[0, s].astype(F32), geo)
    geo = jnp.where(row == 11, 1.0 - 2.0 * (lax.axis_index("y") % 2).astype(F32), geo)
    geo = jnp.where(row == 12, 1.0 - 2.0 * lax.axis_index("core").astype(F32), geo)
    out[GEO:ROWS, :] = geo.astype(BF16)
    copies[1].wait()
    copies[2].wait()


def pack(counts, owned, features, cotangent, offsets):
    smem = pl.BlockSpec(memory_space=pltpu.SMEM)
    hbm = pl.BlockSpec(memory_space=pltpu.HBM)
    return pl.pallas_call(
        pack_kernel,
        out_shape=pltpu.VMEM((ROWS, C), BF16),
        in_specs=[smem, hbm, hbm, hbm, hbm],
        out_specs=HERE,
        scratch_shapes=[pltpu.SMEM((1, 8), jnp.int32), pltpu.VMEM((2, N), BF16), pltpu.SemaphoreType.DMA((4,))],
        compiler_params=LIMIT,
        name="pack",
    )(counts, *(pltpu.with_memory_space_constraint(value, pltpu.HBM) for value in (owned, features, cotangent, offsets)))


def stack_kernel(first, second, third, out):
    out[0:ROWS, :] = first[...]
    out[ROWS : 2 * ROWS, :] = second[...]
    out[2 * ROWS : 3 * ROWS, :] = third[...]


def stacked(first, second, third):
    return pl.pallas_call(
        stack_kernel,
        out_shape=pltpu.VMEM((3 * ROWS, C), BF16),
        in_specs=[HERE] * 3,
        out_specs=HERE,
        compiler_params=LIMIT,
        name="stack",
    )(held(first), held(second), held(third))


def build(cells, own_ref, p_ref, s_ref, store_sums, double_first):
    def rows(step, carry):
        at = pl.multiple_of(step * 16, 16)
        ax = own_ref[pl.ds(at, 16), 0:N]
        ay = own_ref[pl.ds(at, 16), N : 2 * N]
        sums = [None] * K
        for n in range(cells):
            u = p_ref[2 * n : 2 * n + 1, :] - ax
            v = p_ref[2 * n + 1 : 2 * n + 2, :] - ay
            square = u * u + v * v
            t = square * (3.0 * lax.rsqrt(jnp.maximum(square, 1e-30)))
            low = jnp.maximum(1.0 - square, 0.0)
            window = low * low
            if n == 0 and double_first:
                window = window + window
            hats = (
                jnp.maximum(1.0 - t, 0.0),
                jnp.maximum(jnp.minimum(t, 2.0 - t), 0.0),
                jnp.maximum(jnp.minimum(t - 1.0, 3.0 - t), 0.0),
                jnp.maximum(t - 2.0, 0.0),
            )
            for q in range(4):
                weight = window * hats[q]
                for k, term in ((2 * q, weight * u), (2 * q + 1, weight * v)):
                    sums[k] = term if n == 0 else sums[k] + term
                    s_ref[pl.ds(k * N + at, 16), n * N : (n + 1) * N] = term.astype(BF16)
        store_sums(at, sums)
        return carry

    lax.fori_loop(0, N // 16, rows, 0)


def line(block, row):
    return block[row : row + 1, :].astype(F32)


def flag_of(block, at, flip, towards_x, towards_y, right, above):
    def row(dx, dy):
        return line(block, at + FLAG + SLOT[(-flip * dy, flip * dx)])

    def along(dx):
        if not towards_y:
            return row(dx, 0)
        return jnp.where(above, row(dx, towards_y), row(dx, -towards_y))

    if not towards_x:
        return along(0)
    return jnp.where(right, along(towards_x), along(-towards_x))


def place(block, at, use, shift_x, shift_y, p_ref, n):
    p_ref[2 * n : 2 * n + 1, :] = jnp.where(use > 0.5, line(block, at + GEO) + shift_x, -FAR)
    p_ref[2 * n + 1 : 2 * n + 2, :] = line(block, at + GEO + 1) + shift_y


def gather(block, at, x_ref, n):
    x_ref[n * N : (n + 1) * N, 0:C] = block[at : at + N, :]
    x_ref[n * N : (n + 1) * N, C : 2 * C] = block[at + N : at + GEO, :]


def near_kernel(own, narrow0, narrow1, total, sums_out, own_out, s_ref, x_ref, p_ref):
    sy = line(own, SIDES + 1)
    above = sy > 0
    place(own, 0, line(own, LIVE), 0.0, 0.0, p_ref, 0)
    gather(own, 0, x_ref, 0)
    for n, side, block in ((1, 1, narrow0), (2, -1, narrow1)):
        active = flag_of(own, 0, -1, 0, side, None, above) + flag_of(block, 0, 1, 0, side, None, above)
        place(block, 0, line(block, LIVE) * active, 0.0, side * sy, p_ref, n)
        gather(block, 0, x_ref, n)

    own_x = jnp.where(line(own, LIVE) > 0.5, line(own, GEO), FAR)
    own_out[:, 0:N] = jnp.broadcast_to(own_x, (N, N)).T
    own_out[:, N : 2 * N] = jnp.broadcast_to(line(own, GEO + 1), (N, N)).T

    def store_sums(at, sums):
        for k in range(K):
            sums_out[pl.ds(k * N + at, 16), :] = sums[k]

    build(3, own_out, p_ref, s_ref, store_sums, True)
    total[...] = jnp.dot(s_ref[...], x_ref[...], preferred_element_type=F32)


def near(stack):
    return pl.pallas_call(
        near_kernel_stacked,
        out_shape=(
            pltpu.VMEM((K * N, 2 * C), F32),
            pltpu.VMEM((K * N, N), F32),
            pltpu.VMEM((N, 2 * N), F32),
        ),
        in_specs=[HERE],
        out_specs=(HERE,) * 3,
        scratch_shapes=[
            pltpu.VMEM((K * N, 3 * N), BF16),
            pltpu.VMEM((3 * N, 2 * C), BF16),
            pltpu.VMEM((8, N), F32),
        ],
        compiler_params=LIMIT,
        name="near",
    )(held(stack))


def near_kernel_stacked(stack, *refs):
    near_kernel(*(stack.at[i * ROWS : (i + 1) * ROWS] for i in range(3)), *refs)


def far_kernel(stack, total, sums_in, own_at, wide0, wide1, z_ref, w_ref, mine, theirs, s_ref, x_ref, r_ref, t_ref, part, p_ref):
    sx, sy = line(stack, SIDES), line(stack, SIDES + 1)
    right, above = sx > 0, sy > 0
    n = 0
    for i, block in ((1, wide0), (-1, wide1)):
        for j, at in ((0, 0), (1, ROWS), (-1, 2 * ROWS)):
            active = flag_of(stack, at, 1, i, j, right, above) + flag_of(block, 0, -1, i, j, right, above)
            place(block, at, line(block, at + LIVE) * active, i * sx, j * sy, p_ref, n)
            gather(block, at, x_ref, n)
            n += 1

    def store_sums(at, sums):
        for k in range(K):
            both = jnp.sum(sums[k] + sums_in[pl.ds(k * N + at, 16), :], axis=1, keepdims=True)
            r_ref[pl.ds(k * N + at, 16), :] = jnp.broadcast_to(both, (16, N))

    build(6, own_at, p_ref, s_ref, store_sums, False)
    t_ref[...] = jnp.dot(s_ref[...], x_ref[...], preferred_element_type=F32) + total[...]
    f = stack[0:N, :].astype(F32)
    g = stack[N:GEO, :].astype(F32)
    for k in range(K):
        r = r_ref[k * N : (k + 1) * N, :]
        z_ref[:, k * C : (k + 1) * C] = (r * f + t_ref[k * N : (k + 1) * N, 0:C]).astype(BF16)
        w_ref[:, k * C : (k + 1) * C] = (r * g - t_ref[k * N : (k + 1) * N, C : 2 * C]).astype(BF16)
    own_g = stack[N:GEO, :]
    part[...] = lax.dot_general(z_ref[...], own_g, (((0,), (0,)), ((), ())), preferred_element_type=F32).astype(BF16)
    core = lax.axis_index("core")
    mine[...] = part[pl.ds(pl.multiple_of(core * HALF, HALF), HALF), :]
    theirs[...] = part[pl.ds(pl.multiple_of((1 - core) * HALF, HALF), HALF), :]


def join_kernel(mine, given, out):
    at = pl.multiple_of((1 - lax.axis_index("core")) * HALF, HALF)
    out[...] = (mine[...].astype(F32) + given[pl.ds(at, HALF), :].astype(F32)).astype(BF16)


def join(mine, given):
    return pl.pallas_call(
        join_kernel,
        out_shape=pltpu.VMEM((HALF, C), BF16),
        in_specs=[HERE] * 2,
        out_specs=HERE,
        compiler_params=LIMIT,
        name="join",
    )(held(mine), held(given))


def result_kernel(z_ref, w_ref, kernels, corrected, grad):
    force = jnp.dot(z_ref[...], kernels[...], preferred_element_type=F32)
    corrected[...] = (force * KERNEL_SCALE).astype(BF16)
    back = None
    for k in range(K):
        term = lax.dot_general(
            w_ref[:, k * C : (k + 1) * C],
            kernels[k * C : (k + 1) * C, :],
            (((1,), (1,)), ((), ())),
            preferred_element_type=F32,
        )
        back = term if back is None else back + term
    grad[...] = back * KERNEL_SCALE


def results(z, w, kernels):
    return pl.pallas_call(
        result_kernel,
        out_shape=(jax.ShapeDtypeStruct((N, C), BF16), jax.ShapeDtypeStruct((N, C), F32)),
        in_specs=[HERE] * 3,
        out_specs=(HERE,) * 2,
        compiler_params=LIMIT,
        name="results",
    )(*(held(value) for value in (z, w, kernels)))


def far(stack, total, sums, own_at, wide0, wide1):
    return pl.pallas_call(
        far_kernel,
        out_shape=(
            pltpu.VMEM((N, K * C), BF16),
            pltpu.VMEM((N, K * C), BF16),
            pltpu.VMEM((HALF, C), BF16),
            pltpu.VMEM((HALF, C), BF16),
        ),
        in_specs=[HERE] * 6,
        out_specs=(HERE,) * 4,
        scratch_shapes=[
            pltpu.VMEM((K * N, 6 * N), BF16),
            pltpu.VMEM((6 * N, 2 * C), BF16),
            pltpu.VMEM((K * N, N), F32),
            pltpu.VMEM((K * N, 2 * C), F32),
            pltpu.VMEM((K * C, C), BF16),
            pltpu.VMEM((16, N), F32),
        ],
        compiler_params=LIMIT,
        name="far",
    )(*(held(value) for value in (stack, total, sums, own_at, wide0, wide1)))


def swapped(value, axes, second):
    count = lax.axis_size(axes)
    pairs = [(i, (i + 1 if (i + second) % 2 == 0 else i - 1) % count) for i in range(count)]
    return lax.ppermute(value, axes, pairs)


def exchanged(blocks, axes):
    return lax.all_to_all(blocks, axes, 0, 0, tiled=False)


def spread_kernel(blocks, out):
    total = jnp.sum(blocks[...].astype(F32), axis=0).astype(BF16)
    for i in range(out.shape[0]):
        out[i] = total


def spread(blocks, copies):
    return pl.pallas_call(
        spread_kernel,
        out_shape=pltpu.VMEM((copies,) + blocks.shape[1:], BF16),
        in_specs=[HERE],
        out_specs=HERE,
        compiler_params=LIMIT,
        name="spread",
    )(held(blocks))


def whole_sum(part):
    group, depth = lax.axis_size(GROUP), lax.axis_size(DEPTH)
    pieces = exchanged(part.reshape(group, -1, C), GROUP)
    pieces = exchanged(spread(pieces, depth), DEPTH)
    return exchanged(spread(pieces, group), GROUP).reshape(-1, C)


def body(features, offsets, counts, owned_pairs, kernels, cotangent):
    own = pack(counts, owned_pairs[0], features[0, 0], cotangent[0, 0], offsets[0, 0])
    narrow1 = swapped(own, NARROW, 1)
    narrow0 = swapped(own, NARROW, 0)
    stack = stacked(own, narrow0, narrow1)
    wide1 = swapped(stack, WIDE, 1)
    wide0 = swapped(stack, WIDE, 0)
    sums = near(stack)
    z, w, mine, theirs = far(stack, *sums, wide0, wide1)
    given = lax.all_gather(theirs, "core", axis=0, tiled=True)
    corrected, grad = results(z, w, kernels.reshape(K * C, C))
    half = join(mine, given)
    weights = lax.all_gather(whole_sum(half), "core", axis=0, tiled=True)
    scale = KERNEL_SCALE / float(lax.axis_size(WIDE) * lax.axis_size(NARROW) * N) ** 0.5
    weights = (weights.astype(F32) * scale).reshape(K, C, C)
    return corrected[None, None], grad[None, None], weights


def solution(mesh):
    split = Mesh(mesh.devices.reshape(4, 8, 4, 2, 2), ("zl", "y", "x", "zh", "core"))
    cell = P(WIDE, NARROW)
    return jax.shard_map(
        body,
        mesh=split,
        in_specs=(cell, cell, cell, cell, P(), cell),
        out_specs=(cell, cell, P()),
        check_vma=False,
    )
```

time: 99.8 us -> 87.8 us (0.88)
  blocking collectives: 48.2 us -> 35.5 us
  starting transfers between devices: 23.9 us -> 29.6 us
  waiting for transfers between devices: 16.4 us -> 14.3 us
  Pallas kernels: 6.91 us -> 5.79 us
    all_to_all x3 -> x2, blocking collectives: 48.2 us -> 26.1 us  [exchanged(): return lax.all_to_all(blocks, axes, 0, 0, tiled=False)]
    ppermute x4, waiting for transfers between devices: 16.4 us -> 5.94 us  [swapped(): return lax.ppermute(value, axes, pairs)]
    all_gather x0 -> x2, blocking collectives: none -> 9.44 us  [the longest x1 6.32 us: body(): weights = lax.all_gather(whole_sum(half), 'core', axis=0, tiled=True)]
    all_to_all x0 -> x1, waiting for transfers between devices: none -> 8.33 us  [exchanged(): return lax.all_to_all(blocks, axes, 0, 0, tiled=False)]
    all_to_all x0 -> x1, starting transfers between devices: none -> 3.88 us  [exchanged(): return lax.all_to_all(blocks, axes, 0, 0, tiled=False)]
    ppermute x4, starting transfers between devices: 23.9 us -> 25.7 us  [swapped(): return lax.ppermute(value, axes, pairs)]
    pallas_call x2 -> x8, Pallas kernels: 6.91 us -> 5.79 us  [the longest x1 2.18 us: far(): pl.pallas_call(far_kernel, out_shape=(pltpu.VMEM((N, K * C), BF16), pltpu...]
  transfers between devices with their start and end apart: 4 -> 5, of which waited for: 4 -> 4; matrix products, arithmetic and copies ran while one was open for 0% -> 0% of each run, Pallas kernels for 0% -> 2%
where the time goes in v2:
time: 87.8 us; the launch traced here: 87.4 us
  blocking collectives  35.5 us (40%)
  starting transfers between devices  29.6 us (34%)
  waiting for transfers between devices  14.3 us (16%)
  Pallas kernels  5.79 us (7%)
  between operations  1.36 us (2%)
    all_to_all x2, blocking collectives, exchanged(): return lax.all_to_all(blocks, axes, 0, 0, tiled=False)  26.1 us
    ppermute x4, starting transfers between devices, swapped(): return lax.ppermute(value, axes, pairs)  25.7 us
    all_to_all x1, waiting for transfers between devices, exchanged(): return lax.all_to_all(blocks, axes, 0, 0, tiled=False)  8.33 us
    all_gather x1, blocking collectives, body(): weights = lax.all_gather(whole_sum(half), 'core', axis=0, tiled=True)  6.32 us
    ppermute x4, waiting for transfers between devices, swapped(): return lax.ppermute(value, axes, pairs)  5.94 us
    all_to_all x1, starting transfers between devices, exchanged(): return lax.all_to_all(blocks, axes, 0, 0, tiled=False)  3.88 us
    all_gather x1, blocking collectives, body(): given = lax.all_gather(theirs, 'core', axis=0, tiled=True)  3.12 us
    pallas_call x1, Pallas kernels, far(): pl.pallas_call(far_kernel, out_shape=(pltpu.VMEM((N, K * C), BF16), pltpu...  2.18 us
  transfers between devices with their start and end apart: 5, of which 4 were waited for; matrix products, arithmetic and copies ran while one was open for 0% of the time, Pallas kernels for 2%

profile of v2, /device:TPU:1, one launch (start us, length us, event | category | flops | bytes accessed | tf_op | source)
XLA Modules:
  0.0 87.4 jit_solution(18292148633388279550)
XLA Ops:
  1.3 0.9 pack.1.first
  2.1 12.0 %collective-permute-start.1 = (bf16[272,128]{1,0:T(8,128)(2,1)S(1)}, bf16[272,128]{1,0:T(8,128)(2,1)S(1)}, u32[]{:S(2)}, u32[]{:S(2)}) collective-permute-start(bf16[272,128]{1,0:T(8,128)(2,1)S(1)} %pack.1.first), channel_id=1, source_target_pairs={{0,15},{1,2},{2,1},{3,4},{4,3},{5,6},{6,5},{7,8},{8,7},{9,10},{10,... | collective-permute-start | bytes 208904 | tf_op jit(solution)/shard_map/ppermute | solution.py:293
  14.2 3.9 %collective-permute-start = (bf16[272,128]{1,0:T(8,128)(2,1)S(1)}, bf16[272,128]{1,0:T(8,128)(2,1)S(1)}, u32[]{:S(2)}, u32[]{:S(2)}) collective-permute-start(bf16[272,128]{1,0:T(8,128)(2,1)S(1)} %pack.1.first), channel_id=1, source_target_pairs={{0,1},{1,0},{2,3},{3,2},{4,5},{5,4},{6,7},{7,6},{8,9},{9,8},{10,11... | collective-permute-start | bytes 208904 | tf_op jit(solution)/shard_map/ppermute | solution.py:293
  18.1 0.0 collective-permute-done.1.third
  18.1 0.9 %collective-permute-done.second = bf16[272,128]{1,0:T(8,128)(2,1)S(1)} collective-permute-done((bf16[272,128]{1,0:T(8,128)(2,1)S(1)}, bf16[272,128]{1,0:T(8,128)(2,1)S(1)}, u32[]{:S(2)}, u32[]{:S(2)}) %collective-permute-start) | collective-permute-done | bytes 69664 | tf_op jit(solution)/shard_map/ppermute | solution.py:293
  19.0 7.8 %collective-permute-start.3 = (bf16[816,128]{1,0:T(8,128)(2,1)S(1)}, bf16[816,128]{1,0:T(8,128)(2,1)S(1)}, u32[]{:S(2)}, u32[]{:S(2)}) collective-permute-start(bf16[816,128]{1,0:T(8,128)(2,1)S(1)} %stack.1), channel_id=1, source_target_pairs={{0,496},{16,32},{32,16},{48,64},{64,48},{80,96},{96,80},{112,128},... | collective-permute-start | bytes 626696 | tf_op jit(solution)/shard_map/ppermute | solution.py:293
  26.8 1.9 %collective-permute-start.2 = (bf16[816,128]{1,0:T(8,128)(2,1)S(1)}, bf16[816,128]{1,0:T(8,128)(2,1)S(1)}, u32[]{:S(2)}, u32[]{:S(2)}) collective-permute-start(bf16[816,128]{1,0:T(8,128)(2,1)S(1)} %stack.1), channel_id=1, source_target_pairs={{0,16},{16,0},{32,48},{48,32},{64,80},{80,64},{96,112},{112,96},{1... | collective-permute-start | bytes 626696 | tf_op jit(solution)/shard_map/ppermute | solution.py:293
  28.8 1.0 %near.1 = (f32[1024,256]{1,0:T(8,128)S(1)}, f32[1024,128]{1,0:T(8,128)S(1)}, f32[128,256]{1,0:T(8,128)S(1)}) custom-call(bf16[816,128]{1,0:T(8,128)(2,1)S(1)} %stack.1), custom_call_target="tpu_custom_call" | custom-call | tf_op jit(solution)/shard_map/near/pallas_call | solution.py:170
  29.8 1.2 %collective-permute-done.3.wide1 = bf16[816,128]{1,0:T(8,128)(2,1)S(1)} collective-permute-done((bf16[816,128]{1,0:T(8,128)(2,1)S(1)}, bf16[816,128]{1,0:T(8,128)(2,1)S(1)}, u32[]{:S(2)}, u32[]{:S(2)}) %collective-permute-start.3) | collective-permute-done | bytes 208928 | tf_op jit(solution)/shard_map/ppermute | solution.py:293
  31.0 3.8 %collective-permute-done.2.wide0 = bf16[816,128]{1,0:T(8,128)(2,1)S(1)} collective-permute-done((bf16[816,128]{1,0:T(8,128)(2,1)S(1)}, bf16[816,128]{1,0:T(8,128)(2,1)S(1)}, u32[]{:S(2)}, u32[]{:S(2)}) %collective-permute-start.2) | collective-permute-done | bytes 208928 | tf_op jit(solution)/shard_map/ppermute | solution.py:293
  34.8 2.2 %far.1 = (bf16[128,1024]{1,0:T(8,128)(2,1)S(1)}, bf16[128,1024]{1,0:T(8,128)(2,1)S(1)}, bf16[512,128]{1,0:T(8,128)(2,1)S(1)}, bf16[512,128]{1,0:T(8,128)(2,1)S(1)}) custom-call(bf16[816,128]{1,0:T(8,128)(2,1)S(1)} %stack.1, f32[1024,256]{1,0:T(8,128)S(1)} %get-tuple-element.12.total, f32[1024,128]{1,0:T(8,128)S(1)} %get-tuple-element.13.sums_in, ...), custom_call_target="tpu_custom_call" | custom-call | tf_op jit(solution)/shard_map/far/pallas_call | solution.py:267
  37.0 3.1 %all_gather.6.given = bf16[1024,128]{1,0:T(8,128)(2,1)S(1)} all-gather(bf16[512,128]{1,0:T(8,128)(2,1)S(1)} %get-tuple-element.20), channel_id=1, replica_groups=mesh['zl'=4,'y'=8,'x'=4,'zh'=2,'core'=2] {'core'}, dimensions={0}, use_global_device_ids=true | all-gather | bytes 393216 | tf_op jit(solution)/shard_map/all_gather | solution.py:333
  40.2 12.8 %all_to_all.15.blocks = bf16[32,16,128]{2,1,0:T(8,128)(2,1)S(1)} all-to-all(bf16[32,16,128]{2,1,0:T(8,128)(2,1)S(1)} %bitcast.10), channel_id=1, replica_groups=mesh['zl'=4,'y'=8,'x'=4,'zh'=2,'core'=2] {'y','x'}, dimensions={0} | all-to-all | bytes 262144 | tf_op jit(solution)/shard_map/all_to_all | solution.py:297
  53.0 0.0 copy-start
  53.0 13.3 %all_to_all.16.blocks = bf16[8,16,128]{2,1,0:T(8,128)(2,1)S(1)} all-to-all(bf16[8,16,128]{2,1,0:T(8,128)(2,1)S(1)} %spread.2), channel_id=1, replica_groups=mesh['zl'=4,'y'=8,'x'=4,'zh'=2,'core'=2] {'zl','zh'}, dimensions={0} | all-to-all | bytes 65536 | tf_op jit(solution)/shard_map/all_to_all | solution.py:297
  66.3 0.7 spread.3
  67.0 3.9 %all-to-all-start.2 = ((bf16[32,16,128]{2,1,0:T(8,128)(2,1)}), bf16[32,16,128]{2,1,0:T(8,128)(2,1)S(1)}, u32[]{:S(2)}, u32[]{:S(2)}) async-start(bf16[32,16,128]{2,1,0:T(8,128)(2,1)} %spread.3), calls=%async_computation.2 | async-start | bytes 262144 | tf_op jit(solution)/shard_map/all_to_all | solution.py:297
  70.9 0.0 copy-done
  70.9 1.0 %results.1 = (bf16[128,128]{1,0:T(8,128)(2,1)}, f32[128,128]{1,0:T(8,128)}) custom-call(bf16[128,1024]{1,0:T(8,128)(2,1)S(1)} %get-tuple-element.15.z_ref, bf16[128,1024]{1,0:T(8,128)(2,1)S(1)} %get-tuple-element.16.w_ref, bf16[1024,128]{1,0:T(8,128)(2,1)S(1)} %bitcast.11), custom_call_target="tpu_custom_call" | custom-call | tf_op jit(solution)/shard_map/results/pallas_call | solution.py:256
  71.9 8.3 %all-to-all-done.2 = bf16[32,16,128]{2,1,0:T(8,128)(2,1)S(1)} async-done(((bf16[32,16,128]{2,1,0:T(8,128)(2,1)}), bf16[32,16,128]{2,1,0:T(8,128)(2,1)S(1)}, u32[]{:S(2)}, u32[]{:S(2)}) %all-to-all-start.2) | async-done | bytes 131104 | tf_op jit(solution)/shard_map/all_to_all | solution.py:297
  80.2 6.3 %all_gather.7 = bf16[1024,128]{1,0:T(8,128)(2,1)S(1)} all-gather(bf16[512,128]{1,0:T(8,128)(2,1)S(1)} %bitcast.12), channel_id=1, replica_groups=mesh['zl'=4,'y'=8,'x'=4,'zh'=2,'core'=2] {'core'}, dimensions={0}, use_global_device_ids=true | all-gather | bytes 393216 | tf_op jit(solution)/shard_map/all_gather | solution.py:336
  86.5 0.8 convert_multiply_fusion
  (3 shorter events, 0.1 us)
Async XLA Ops:
  2.1 16.0 %collective-permute-start.1 = (bf16[272,128]{1,0:T(8,128)(2,1)S(1)}, bf16[272,128]{1,0:T(8,128)(2,1)S(1)}, u32[]{:S(2)}, u32[]{:S(2)}) collective-permute-start(bf16[272,128]{1,0:T(8,128)(2,1)S(1)} %pack.1.first), channel_id=1, source_target_pairs={{0,15},{1,2},{2,1},{3,4},{4,3},{5,6},{6,5},{7,8},{8,7},{9,10},{10,... | collective-permute-start | bytes 208904 | tf_op jit(solution)/shard_map/ppermute | solution.py:293
  14.2 4.8 %collective-permute-start = (bf16[272,128]{1,0:T(8,128)(2,1)S(1)}, bf16[272,128]{1,0:T(8,128)(2,1)S(1)}, u32[]{:S(2)}, u32[]{:S(2)}) collective-permute-start(bf16[272,128]{1,0:T(8,128)(2,1)S(1)} %pack.1.first), channel_id=1, source_target_pairs={{0,1},{1,0},{2,3},{3,2},{4,5},{5,4},{6,7},{7,6},{8,9},{9,8},{10,11... | collective-permute-start | bytes 208904 | tf_op jit(solution)/shard_map/ppermute | solution.py:293
  19.0 12.0 %collective-permute-start.3 = (bf16[816,128]{1,0:T(8,128)(2,1)S(1)}, bf16[816,128]{1,0:T(8,128)(2,1)S(1)}, u32[]{:S(2)}, u32[]{:S(2)}) collective-permute-start(bf16[816,128]{1,0:T(8,128)(2,1)S(1)} %stack.1), channel_id=1, source_target_pairs={{0,496},{16,32},{32,16},{48,64},{64,48},{80,96},{96,80},{112,128},... | collective-permute-start | bytes 626696 | tf_op jit(solution)/shard_map/ppermute | solution.py:293
  26.8 8.0 %collective-permute-start.2 = (bf16[816,128]{1,0:T(8,128)(2,1)S(1)}, bf16[816,128]{1,0:T(8,128)(2,1)S(1)}, u32[]{:S(2)}, u32[]{:S(2)}) collective-permute-start(bf16[816,128]{1,0:T(8,128)(2,1)S(1)} %stack.1), channel_id=1, source_target_pairs={{0,16},{16,0},{32,48},{48,32},{64,80},{80,64},{96,112},{112,96},{1... | collective-permute-start | bytes 626696 | tf_op jit(solution)/shard_map/ppermute | solution.py:293
  53.0 17.9 %copy-start = (bf16[8,128,128]{2,1,0:T(8,128)(2,1)S(1)}, bf16[8,128,128]{2,1,0:T(8,128)(2,1)}, u32[]{:S(2)}) copy-start(bf16[8,128,128]{2,1,0:T(8,128)(2,1)} %param.10) | copy-start | bytes 786436
  67.0 13.2 %all-to-all-start.2 = ((bf16[32,16,128]{2,1,0:T(8,128)(2,1)}), bf16[32,16,128]{2,1,0:T(8,128)(2,1)S(1)}, u32[]{:S(2)}, u32[]{:S(2)}) async-start(bf16[32,16,128]{2,1,0:T(8,128)(2,1)} %spread.3), calls=%async_computation.2 | async-start | bytes 262144 | tf_op jit(solution)/shard_map/all_to_all | solution.py:297

commit v3 on v2

--- a/solution.py
+++ b/solution.py
@@ -11,8 +11,8 @@
 KERNEL_SCALE = 0.0625
 FAR = 64.0
 K, N, C = 8, 128, 128
-GEO = 2 * N
-ROWS = 2 * N + 16
+GEO = N
+ROWS = N + 16
 HALF = K * C // 2
 LIVE, FLAG, SIDES = GEO + 2, GEO + 3, GEO + 11
 WIDE = ("zl", "y")
@@ -32,7 +32,7 @@
     copies = (
         pltpu.make_async_copy(offsets, off_ref, sems.at[0]),
         pltpu.make_async_copy(features, out.at[0:N], sems.at[1]),
-        pltpu.make_async_copy(cotangent, out.at[N:GEO], sems.at[2]),
+        pltpu.make_async_copy(cotangent, out.at[ROWS : ROWS + N], sems.at[2]),
         pltpu.make_async_copy(owned_hbm, owned, sems.at[3]),
     )
     for copy in copies:
@@ -58,7 +58,7 @@
     hbm = pl.BlockSpec(memory_space=pltpu.HBM)
     return pl.pallas_call(
         pack_kernel,
-        out_shape=pltpu.VMEM((ROWS, C), BF16),
+        out_shape=pltpu.VMEM((ROWS + N, C), BF16),
         in_specs=[smem, hbm, hbm, hbm, hbm],
         out_specs=HERE,
         scratch_shapes=[pltpu.SMEM((1, 8), jnp.int32), pltpu.VMEM((2, N), BF16), pltpu.SemaphoreType.DMA((4,))],
@@ -67,18 +67,18 @@
     )(counts, *(pltpu.with_memory_space_constraint(value, pltpu.HBM) for value in (owned, features, cotangent, offsets)))
 
 
-def stack_kernel(first, second, third, out):
-    out[0:ROWS, :] = first[...]
-    out[ROWS : 2 * ROWS, :] = second[...]
-    out[2 * ROWS : 3 * ROWS, :] = third[...]
+def stack_kernel(first, second, third, out, out_g):
+    for i, block in enumerate((first, second, third)):
+        out[i * ROWS : (i + 1) * ROWS, :] = block[0:ROWS, :]
+        out_g[i * N : (i + 1) * N, :] = block[ROWS : ROWS + N, :]
 
 
 def stacked(first, second, third):
     return pl.pallas_call(
         stack_kernel,
-        out_shape=pltpu.VMEM((3 * ROWS, C), BF16),
+        out_shape=(pltpu.VMEM((3 * ROWS, C), BF16), pltpu.VMEM((3 * N, C), BF16)),
         in_specs=[HERE] * 3,
-        out_specs=HERE,
+        out_specs=(HERE,) * 2,
         compiler_params=LIMIT,
         name="stack",
     )(held(first), held(second), held(third))
@@ -140,11 +140,10 @@
 
 
 def gather(block, at, x_ref, n):
-    x_ref[n * N : (n + 1) * N, 0:C] = block[at : at + N, :]
-    x_ref[n * N : (n + 1) * N, C : 2 * C] = block[at + N : at + GEO, :]
-
-
-def near_kernel(own, narrow0, narrow1, total, sums_out, own_out, s_ref, x_ref, p_ref):
+    x_ref[n * N : (n + 1) * N, :] = block[at : at + N, :]
+
+
+def near_kernel(own, narrow0, narrow1, total, s_ref, sums_out, own_out, x_ref, p_ref):
     sy = line(own, SIDES + 1)
     above = sy > 0
     place(own, 0, line(own, LIVE), 0.0, 0.0, p_ref, 0)
@@ -170,15 +169,15 @@
     return pl.pallas_call(
         near_kernel_stacked,
         out_shape=(
-            pltpu.VMEM((K * N, 2 * C), F32),
+            pltpu.VMEM((K * N, C), F32),
+            pltpu.VMEM((K * N, 3 * N), BF16),
             pltpu.VMEM((K * N, N), F32),
             pltpu.VMEM((N, 2 * N), F32),
         ),
         in_specs=[HERE],
-        out_specs=(HERE,) * 3,
+        out_specs=(HERE,) * 4,
         scratch_shapes=[
-            pltpu.VMEM((K * N, 3 * N), BF16),
-            pltpu.VMEM((3 * N, 2 * C), BF16),
+            pltpu.VMEM((3 * N, C), BF16),
             pltpu.VMEM((8, N), F32),
         ],
         compiler_params=LIMIT,
@@ -190,7 +189,7 @@
     near_kernel(*(stack.at[i * ROWS : (i + 1) * ROWS] for i in range(3)), *refs)
 
 
-def far_kernel(stack, total, sums_in, own_at, wide0, wide1, z_ref, w_ref, mine, theirs, s_ref, x_ref, r_ref, t_ref, part, p_ref):
+def far_kernel(stack, total, sums_in, own_at, wide0, wide1, stack_g, z_ref, s_ref, r_ref, mine, theirs, x_ref, t_ref, part, p_ref):
     sx, sy = line(stack, SIDES), line(stack, SIDES + 1)
     right, above = sx > 0, sy > 0
     n = 0
@@ -209,13 +208,10 @@
     build(6, own_at, p_ref, s_ref, store_sums, False)
     t_ref[...] = jnp.dot(s_ref[...], x_ref[...], preferred_element_type=F32) + total[...]
     f = stack[0:N, :].astype(F32)
-    g = stack[N:GEO, :].astype(F32)
     for k in range(K):
         r = r_ref[k * N : (k + 1) * N, :]
-        z_ref[:, k * C : (k + 1) * C] = (r * f + t_ref[k * N : (k + 1) * N, 0:C]).astype(BF16)
-        w_ref[:, k * C : (k + 1) * C] = (r * g - t_ref[k * N : (k + 1) * N, C : 2 * C]).astype(BF16)
-    own_g = stack[N:GEO, :]
-    part[...] = lax.dot_general(z_ref[...], own_g, (((0,), (0,)), ((), ())), preferred_element_type=F32).astype(BF16)
+        z_ref[:, k * C : (k + 1) * C] = (r * f + t_ref[k * N : (k + 1) * N, :]).astype(BF16)
+    part[...] = lax.dot_general(z_ref[...], stack_g[0:N, :], (((0,), (0,)), ((), ())), preferred_element_type=F32).astype(BF16)
     core = lax.axis_index("core")
     mine[...] = part[pl.ds(pl.multiple_of(core * HALF, HALF), HALF), :]
     theirs[...] = part[pl.ds(pl.multiple_of((1 - core) * HALF, HALF), HALF), :]
@@ -237,54 +233,57 @@
     )(held(mine), held(given))
 
 
-def result_kernel(z_ref, w_ref, kernels, corrected, grad):
+def result_kernel(z_ref, near_s, far_s, r_ref, own, wide0, wide1, kernels, corrected, grad, t_ref):
     force = jnp.dot(z_ref[...], kernels[...], preferred_element_type=F32)
     corrected[...] = (force * KERNEL_SCALE).astype(BF16)
+    t_ref[...] = (
+        jnp.dot(near_s[...], own[...], preferred_element_type=F32)
+        + jnp.dot(far_s[:, 0 : 3 * N], wide0[...], preferred_element_type=F32)
+        + jnp.dot(far_s[:, 3 * N : 6 * N], wide1[...], preferred_element_type=F32)
+    )
+    g = own[0:N, :].astype(F32)
     back = None
     for k in range(K):
-        term = lax.dot_general(
-            w_ref[:, k * C : (k + 1) * C],
-            kernels[k * C : (k + 1) * C, :],
-            (((1,), (1,)), ((), ())),
-            preferred_element_type=F32,
-        )
+        at = slice(k * N, (k + 1) * N)
+        w = (r_ref[at, :] * g - t_ref[at, :]).astype(BF16)
+        term = lax.dot_general(w, kernels[at, :], (((1,), (1,)), ((), ())), preferred_element_type=F32)
         back = term if back is None else back + term
     grad[...] = back * KERNEL_SCALE
 
 
-def results(z, w, kernels):
+def results(*values):
     return pl.pallas_call(
         result_kernel,
         out_shape=(jax.ShapeDtypeStruct((N, C), BF16), jax.ShapeDtypeStruct((N, C), F32)),
-        in_specs=[HERE] * 3,
+        in_specs=[HERE] * 8,
         out_specs=(HERE,) * 2,
+        scratch_shapes=[pltpu.VMEM((K * N, C), F32)],
         compiler_params=LIMIT,
         name="results",
-    )(*(held(value) for value in (z, w, kernels)))
-
-
-def far(stack, total, sums, own_at, wide0, wide1):
+    )(*(held(value) for value in values))
+
+
+def far(*values):
     return pl.pallas_call(
         far_kernel,
         out_shape=(
             pltpu.VMEM((N, K * C), BF16),
-            pltpu.VMEM((N, K * C), BF16),
+            pltpu.VMEM((K * N, 6 * N), BF16),
+            pltpu.VMEM((K * N, N), F32),
             pltpu.VMEM((HALF, C), BF16),
             pltpu.VMEM((HALF, C), BF16),
         ),
-        in_specs=[HERE] * 6,
-        out_specs=(HERE,) * 4,
+        in_specs=[HERE] * 7,
+        out_specs=(HERE,) * 5,
         scratch_shapes=[
-            pltpu.VMEM((K * N, 6 * N), BF16),
-            pltpu.VMEM((6 * N, 2 * C), BF16),
-            pltpu.VMEM((K * N, N), F32),
-            pltpu.VMEM((K * N, 2 * C), F32),
+            pltpu.VMEM((6 * N, C), BF16),
+            pltpu.VMEM((K * N, C), F32),
             pltpu.VMEM((K * C, C), BF16),
             pltpu.VMEM((16, N), F32),
         ],
         compiler_params=LIMIT,
         name="far",
-    )(*(held(value) for value in (stack, total, sums, own_at, wide0, wide1)))
+    )(*(held(value) for value in values))
 
 
 def swapped(value, axes, second):
@@ -317,23 +316,26 @@
 def whole_sum(part):
     group, depth = lax.axis_size(GROUP), lax.axis_size(DEPTH)
     pieces = exchanged(part.reshape(group, -1, C), GROUP)
-    pieces = exchanged(spread(pieces, depth), DEPTH)
-    return exchanged(spread(pieces, group), GROUP).reshape(-1, C)
+    pieces = spread(pieces, depth)
+    pieces = exchanged(pieces, DEPTH)
+    pieces = spread(pieces, group)
+    return exchanged(pieces, GROUP).reshape(-1, C)
 
 
 def body(features, offsets, counts, owned_pairs, kernels, cotangent):
     own = pack(counts, owned_pairs[0], features[0, 0], cotangent[0, 0], offsets[0, 0])
     narrow1 = swapped(own, NARROW, 1)
     narrow0 = swapped(own, NARROW, 0)
-    stack = stacked(own, narrow0, narrow1)
+    stack, stack_g = stacked(own, narrow0, narrow1)
     wide1 = swapped(stack, WIDE, 1)
     wide0 = swapped(stack, WIDE, 0)
-    sums = near(stack)
-    z, w, mine, theirs = far(stack, *sums, wide0, wide1)
+    total, near_s, sums, own_at = near(stack)
+    z, far_s, r, mine, theirs = far(stack, total, sums, own_at, wide0, wide1, stack_g)
     given = lax.all_gather(theirs, "core", axis=0, tiled=True)
-    corrected, grad = results(z, w, kernels.reshape(K * C, C))
-    half = join(mine, given)
-    weights = lax.all_gather(whole_sum(half), "core", axis=0, tiled=True)
+    weights = lax.all_gather(whole_sum(join(mine, given)), "core", axis=0, tiled=True)
+    wide1_g = swapped(stack_g, WIDE, 1)
+    wide0_g = swapped(stack_g, WIDE, 0)
+    corrected, grad = results(z, near_s, far_s, r, stack_g, wide0_g, wide1_g, kernels.reshape(K * C, C))
     scale = KERNEL_SCALE / float(lax.axis_size(WIDE) * lax.axis_size(NARROW) * N) ** 0.5
     weights = (weights.astype(F32) * scale).reshape(K, C, C)
     return corrected[None, None], grad[None, None], weights

time: 87.8 us -> 94.8 us (1.080)
  starting transfers between devices: 29.6 us -> 35.4 us
  blocking collectives: 35.5 us -> 39.7 us
  waiting for transfers between devices: 14.3 us -> 10.5 us
    all_to_all x1, waiting for transfers between devices: 8.33 us -> 0.01 us  [exchanged(): return lax.all_to_all(blocks, axes, 0, 0, tiled=False)]
    ppermute x4 -> x6, starting transfers between devices: 25.7 us -> 30.8 us  [swapped(): return lax.ppermute(value, axes, pairs)]
    ppermute x4 -> x6, waiting for transfers between devices: 5.94 us -> 10.5 us  [swapped(): return lax.ppermute(value, axes, pairs)]
    all_gather x1, blocking collectives: 3.12 us -> 5.32 us  [body(): given = lax.all_gather(theirs, 'core', axis=0, tiled=True)]
    all_to_all x2, blocking collectives: 26.1 us -> 27.8 us  [exchanged(): return lax.all_to_all(blocks, axes, 0, 0, tiled=False)]
  transfers between devices with their start and end apart: 5 -> 7, of which waited for: 4 -> 3; matrix products, arithmetic and copies ran while one was open for 0% -> 0% of each run, Pallas kernels for 2% -> 3%
where the time goes in v3:
time: 94.8 us; the launch traced here: 94.3 us
  blocking collectives  39.7 us (42%)
  starting transfers between devices  35.4 us (37%)
  waiting for transfers between devices  10.5 us (11%)
  Pallas kernels  6.39 us (7%)
  between operations  1.39 us (1%)
    ppermute x6, starting transfers between devices, swapped(): return lax.ppermute(value, axes, pairs)  30.8 us
    all_to_all x2, blocking collectives, exchanged(): return lax.all_to_all(blocks, axes, 0, 0, tiled=False)  27.8 us
    ppermute x6, waiting for transfers between devices, swapped(): return lax.ppermute(value, axes, pairs)  10.5 us
    all_gather x1, blocking collectives, body(): lax.all_gather(whole_sum(join(mine, given)), 'core', axis=0, tiled=True)  6.57 us
    all_gather x1, blocking collectives, body(): given = lax.all_gather(theirs, 'core', axis=0, tiled=True)  5.32 us
    all_to_all x1, starting transfers between devices, exchanged(): return lax.all_to_all(blocks, axes, 0, 0, tiled=False)  4.58 us
    pallas_call x1, Pallas kernels, far(): pl.pallas_call(far_kernel, out_shape=(pltpu.VMEM((N, K * C), BF16), pltpu...  2.13 us
  transfers between devices with their start and end apart: 7, of which 3 were waited for; matrix products, arithmetic and copies ran while one was open for 0% of the time, Pallas kernels for 3%

profile of v3, /device:TPU:1, one launch (start us, length us, event | category | flops | bytes accessed | tf_op | source)
XLA Modules:
  0.0 94.3 jit_solution(7967164789629775900)
XLA Ops:
  1.3 0.9 pack.1.first
  2.1 8.7 %collective-permute-start = (bf16[272,128]{1,0:T(8,128)(2,1)S(1)}, bf16[272,128]{1,0:T(8,128)(2,1)S(1)}, u32[]{:S(2)}, u32[]{:S(2)}) collective-permute-start(bf16[272,128]{1,0:T(8,128)(2,1)S(1)} %pack.1.first), channel_id=1, source_target_pairs={{0,1},{1,0},{2,3},{3,2},{4,5},{5,4},{6,7},{7,6},{8,9},{9,8},{10,11... | collective-permute-start | bytes 208904 | tf_op jit(solution)/shard_map/ppermute | solution.py:292
  10.9 5.2 %collective-permute-start.1 = (bf16[272,128]{1,0:T(8,128)(2,1)S(1)}, bf16[272,128]{1,0:T(8,128)(2,1)S(1)}, u32[]{:S(2)}, u32[]{:S(2)}) collective-permute-start(bf16[272,128]{1,0:T(8,128)(2,1)S(1)} %pack.1.first), channel_id=1, source_target_pairs={{0,15},{1,2},{2,1},{3,4},{4,3},{5,6},{6,5},{7,8},{8,7},{9,10},{10,... | collective-permute-start | bytes 208904 | tf_op jit(solution)/shard_map/ppermute | solution.py:292
  16.1 0.0 collective-permute-done.second
  16.1 4.3 %collective-permute-done.1.third = bf16[272,128]{1,0:T(8,128)(2,1)S(1)} collective-permute-done((bf16[272,128]{1,0:T(8,128)(2,1)S(1)}, bf16[272,128]{1,0:T(8,128)(2,1)S(1)}, u32[]{:S(2)}, u32[]{:S(2)}) %collective-permute-start.1) | collective-permute-done | bytes 69664 | tf_op jit(solution)/shard_map/ppermute | solution.py:292
  20.4 1.9 %collective-permute-start.2 = (bf16[432,128]{1,0:T(8,128)(2,1)S(1)}, bf16[432,128]{1,0:T(8,128)(2,1)S(1)}, u32[]{:S(2)}, u32[]{:S(2)}) collective-permute-start(bf16[432,128]{1,0:T(8,128)(2,1)S(1)} %get-tuple-element.16.stack), channel_id=1, source_target_pairs={{0,16},{16,0},{32,48},{48,32},{64,80},{80,64},{96,112},{112,96},{1... | collective-permute-start | bytes 331784 | tf_op jit(solution)/shard_map/ppermute | solution.py:292
  22.4 7.2 %collective-permute-start.3 = (bf16[432,128]{1,0:T(8,128)(2,1)S(1)}, bf16[432,128]{1,0:T(8,128)(2,1)S(1)}, u32[]{:S(2)}, u32[]{:S(2)}) collective-permute-start(bf16[432,128]{1,0:T(8,128)(2,1)S(1)} %get-tuple-element.16.stack), channel_id=1, source_target_pairs={{0,496},{16,32},{32,16},{48,64},{64,48},{80,96},{96,80},{112,128},... | collective-permute-start | bytes 331784 | tf_op jit(solution)/shard_map/ppermute | solution.py:292
  29.6 0.9 near.1
  30.5 0.0 collective-permute-done.2.wide0
  30.5 1.2 %collective-permute-done.3.wide1 = bf16[432,128]{1,0:T(8,128)(2,1)S(1)} collective-permute-done((bf16[432,128]{1,0:T(8,128)(2,1)S(1)}, bf16[432,128]{1,0:T(8,128)(2,1)S(1)}, u32[]{:S(2)}, u32[]{:S(2)}) %collective-permute-start.3) | collective-permute-done | bytes 110624 | tf_op jit(solution)/shard_map/ppermute | solution.py:292
  31.8 0.0 copy-start
  31.8 2.1 %far.1 = (bf16[128,1024]{1,0:T(8,128)(2,1)S(1)}, bf16[1024,768]{1,0:T(8,128)(2,1)S(1)}, f32[1024,128]{1,0:T(8,128)S(1)}, bf16[512,128]{1,0:T(8,128)(2,1)S(1)}, bf16[512,128]{1,0:T(8,128)(2,1)S(1)}) custom-call(bf16[432,128]{1,0:T(8,128)(2,1)S(1)} %get-tuple-element.16.stack, f32[1024,128]{1,0:T(8,128)S(1)} %get-tuple-element.17.total, ...), custom_call_target="tpu_custom_call" | custom-call | tf_op jit(solution)/shard_map/far/pallas_call | solution.py:267
  33.9 5.3 %all_gather.6.given = bf16[1024,128]{1,0:T(8,128)(2,1)S(1)} all-gather(bf16[512,128]{1,0:T(8,128)(2,1)S(1)} %get-tuple-element.28), channel_id=1, replica_groups=mesh['zl'=4,'y'=8,'x'=4,'zh'=2,'core'=2] {'core'}, dimensions={0}, use_global_device_ids=true | all-gather | bytes 393216 | tf_op jit(solution)/shard_map/all_gather | solution.py:334
  39.3 13.0 %all_to_all.15.blocks = bf16[32,16,128]{2,1,0:T(8,128)(2,1)S(1)} all-to-all(bf16[32,16,128]{2,1,0:T(8,128)(2,1)S(1)} %bitcast.10), channel_id=1, replica_groups=mesh['zl'=4,'y'=8,'x'=4,'zh'=2,'core'=2] {'y','x'}, dimensions={0} | all-to-all | bytes 262144 | tf_op jit(solution)/shard_map/all_to_all | solution.py:296
  52.3 14.8 %all_to_all.16.blocks = bf16[8,16,128]{2,1,0:T(8,128)(2,1)S(1)} all-to-all(bf16[8,16,128]{2,1,0:T(8,128)(2,1)S(1)} %spread.2), channel_id=1, replica_groups=mesh['zl'=4,'y'=8,'x'=4,'zh'=2,'core'=2] {'zl','zh'}, dimensions={0} | all-to-all | bytes 65536 | tf_op jit(solution)/shard_map/all_to_all | solution.py:296
  67.1 0.7 spread.3
  67.8 4.6 %all-to-all-start.2 = ((bf16[32,16,128]{2,1,0:T(8,128)(2,1)}), bf16[32,16,128]{2,1,0:T(8,128)(2,1)}, u32[]{:S(2)}, u32[]{:S(2)}) async-start(bf16[32,16,128]{2,1,0:T(8,128)(2,1)} %spread.3), calls=%async_computation.2 | async-start | bytes 262144 | tf_op jit(solution)/shard_map/all_to_all | solution.py:296
  72.4 3.0 %collective-permute-start.4 = (bf16[384,128]{1,0:T(8,128)(2,1)S(1)}, bf16[384,128]{1,0:T(8,128)(2,1)S(1)}, u32[]{:S(2)}, u32[]{:S(2)}) collective-permute-start(bf16[384,128]{1,0:T(8,128)(2,1)S(1)} %get-tuple-element.20.stack_g.own), channel_id=1, source_target_pairs={{0,16},{16,0},{32,48},{48,32},{64,80},{80,64},{96,112},{112,96},{1... | collective-permute-start | bytes 294920 | tf_op jit(solution)/shard_map/ppermute | solution.py:292
  75.4 4.8 %collective-permute-start.5 = (bf16[384,128]{1,0:T(8,128)(2,1)S(1)}, bf16[384,128]{1,0:T(8,128)(2,1)S(1)}, u32[]{:S(2)}, u32[]{:S(2)}) collective-permute-start(bf16[384,128]{1,0:T(8,128)(2,1)S(1)} %get-tuple-element.20.stack_g.own), channel_id=1, source_target_pairs={{0,496},{16,32},{32,16},{48,64},{64,48},{80,96},{96,80},{112,128},... | collective-permute-start | bytes 294920 | tf_op jit(solution)/shard_map/ppermute | solution.py:292
  80.2 0.0 collective-permute-done.4.wide0
  80.2 5.0 %collective-permute-done.5.wide1 = bf16[384,128]{1,0:T(8,128)(2,1)S(1)} collective-permute-done((bf16[384,128]{1,0:T(8,128)(2,1)S(1)}, bf16[384,128]{1,0:T(8,128)(2,1)S(1)}, u32[]{:S(2)}, u32[]{:S(2)}) %collective-permute-start.5) | collective-permute-done | bytes 98336 | tf_op jit(solution)/shard_map/ppermute | solution.py:292
  85.1 0.0 copy-done
  85.1 1.8 %results.1 = (bf16[128,128]{1,0:T(8,128)(2,1)}, f32[128,128]{1,0:T(8,128)}) custom-call(bf16[128,1024]{1,0:T(8,128)(2,1)S(1)} %get-tuple-element.21.z_ref, bf16[1024,384]{1,0:T(8,128)(2,1)S(1)} %get-tuple-element.22.near_s, bf16[1024,768]{1,0:T(8,128)(2,1)S(1)} %get-tuple-element.23.far_s, f32[1024,128]{1,0:T(8,128)S(1)} %get-tuple-element.24.r_ref, ...), custom_call_target="tpu_custom_call" | custom-call | tf_op jit(solution)/shard_map/results/pallas_call | solution.py:255
  86.9 0.0 all-to-all-done.2
  86.9 6.6 %all_gather.7 = bf16[1024,128]{1,0:T(8,128)(2,1)S(1)} all-gather(bf16[512,128]{1,0:T(8,128)(2,1)} %bitcast.8), channel_id=1, replica_groups=mesh['zl'=4,'y'=8,'x'=4,'zh'=2,'core'=2] {'core'}, dimensions={0}, use_global_device_ids=true | all-gather | bytes 393216 | tf_op jit(solution)/shard_map/all_gather | solution.py:335
  93.5 0.8 convert_multiply_fusion
  (3 shorter events, 0.1 us)
Async XLA Ops:
  2.1 14.0 %collective-permute-start = (bf16[272,128]{1,0:T(8,128)(2,1)S(1)}, bf16[272,128]{1,0:T(8,128)(2,1)S(1)}, u32[]{:S(2)}, u32[]{:S(2)}) collective-permute-start(bf16[272,128]{1,0:T(8,128)(2,1)S(1)} %pack.1.first), channel_id=1, source_target_pairs={{0,1},{1,0},{2,3},{3,2},{4,5},{5,4},{6,7},{7,6},{8,9},{9,8},{10,11... | collective-permute-start | bytes 208904 | tf_op jit(solution)/shard_map/ppermute | solution.py:292
  10.9 9.5 %collective-permute-start.1 = (bf16[272,128]{1,0:T(8,128)(2,1)S(1)}, bf16[272,128]{1,0:T(8,128)(2,1)S(1)}, u32[]{:S(2)}, u32[]{:S(2)}) collective-permute-start(bf16[272,128]{1,0:T(8,128)(2,1)S(1)} %pack.1.first), channel_id=1, source_target_pairs={{0,15},{1,2},{2,1},{3,4},{4,3},{5,6},{6,5},{7,8},{8,7},{9,10},{10,... | collective-permute-start | bytes 208904 | tf_op jit(solution)/shard_map/ppermute | solution.py:292
  20.4 10.1 %collective-permute-start.2 = (bf16[432,128]{1,0:T(8,128)(2,1)S(1)}, bf16[432,128]{1,0:T(8,128)(2,1)S(1)}, u32[]{:S(2)}, u32[]{:S(2)}) collective-permute-start(bf16[432,128]{1,0:T(8,128)(2,1)S(1)} %get-tuple-element.16.stack), channel_id=1, source_target_pairs={{0,16},{16,0},{32,48},{48,32},{64,80},{80,64},{96,112},{112,96},{1... | collective-permute-start | bytes 331784 | tf_op jit(solution)/shard_map/ppermute | solution.py:292
  22.4 9.4 %collective-permute-start.3 = (bf16[432,128]{1,0:T(8,128)(2,1)S(1)}, bf16[432,128]{1,0:T(8,128)(2,1)S(1)}, u32[]{:S(2)}, u32[]{:S(2)}) collective-permute-start(bf16[432,128]{1,0:T(8,128)(2,1)S(1)} %get-tuple-element.16.stack), channel_id=1, source_target_pairs={{0,496},{16,32},{32,16},{48,64},{64,48},{80,96},{96,80},{112,128},... | collective-permute-start | bytes 331784 | tf_op jit(solution)/shard_map/ppermute | solution.py:292
  31.8 53.4 %copy-start = (bf16[8,128,128]{2,1,0:T(8,128)(2,1)S(1)}, bf16[8,128,128]{2,1,0:T(8,128)(2,1)}, u32[]{:S(2)}) copy-start(bf16[8,128,128]{2,1,0:T(8,128)(2,1)} %param.10) | copy-start | bytes 786436
  67.8 19.1 %all-to-all-start.2 = ((bf16[32,16,128]{2,1,0:T(8,128)(2,1)}), bf16[32,16,128]{2,1,0:T(8,128)(2,1)}, u32[]{:S(2)}, u32[]{:S(2)}) async-start(bf16[32,16,128]{2,1,0:T(8,128)(2,1)} %spread.3), calls=%async_computation.2 | async-start | bytes 262144 | tf_op jit(solution)/shard_map/all_to_all | solution.py:296
  72.4 7.8 %collective-permute-start.4 = (bf16[384,128]{1,0:T(8,128)(2,1)S(1)}, bf16[384,128]{1,0:T(8,128)(2,1)S(1)}, u32[]{:S(2)}, u32[]{:S(2)}) collective-permute-start(bf16[384,128]{1,0:T(8,128)(2,1)S(1)} %get-tuple-element.20.stack_g.own), channel_id=1, source_target_pairs={{0,16},{16,0},{32,48},{48,32},{64,80},{80,64},{96,112},{112,96},{1... | collective-permute-start | bytes 294920 | tf_op jit(solution)/shard_map/ppermute | solution.py:292
  75.4 9.8 %collective-permute-start.5 = (bf16[384,128]{1,0:T(8,128)(2,1)S(1)}, bf16[384,128]{1,0:T(8,128)(2,1)S(1)}, u32[]{:S(2)}, u32[]{:S(2)}) collective-permute-start(bf16[384,128]{1,0:T(8,128)(2,1)S(1)} %get-tuple-element.20.stack_g.own), channel_id=1, source_target_pairs={{0,496},{16,32},{32,16},{48,64},{64,48},{80,96},{96,80},{112,128},... | collective-permute-start | bytes 294920 | tf_op jit(solution)/shard_map/ppermute | solution.py:292
